TPU v7x, 256 devices: a whole 4x4x8 slice. The times are simulated.
256 devices in a mesh: dp: 8 (over z_lo, core), heads: 32 (over y, x, z_hi).
Axes of the slice: x: 4, y: 4, z: 8 (z_hi: 2, z_lo: 4; z = z_hi * 4 + z_lo), core: 2. Of those that a mesh axis runs over, the one named last changes fastest.
Arguments:
- latent: bfloat16 [8, 1024, 512], P(None, 'dp'), may hold values from -6 to 6
- rope_keys: bfloat16 [8, 1024, 64], P(None, 'dp'), may hold values from -6 to 6
- queries: bfloat16 [8, 1024, 24576], P(None, 'dp', 'heads'), may hold values from -320 to 320
- grad_out: bfloat16 [8, 1024, 16384], P(None, 'dp', 'heads'), may hold values from -2 to 2
- key_value_up_weight: bfloat16 [8, 512, 32768], P('dp', None, 'heads'), may hold values from -0.25 to 0.25
- momentum: bfloat16 [8, 512, 32768], P('dp', None, 'heads'), may hold values from -16 to 16
Outputs:
- new_momentum: bfloat16 [8, 512, 32768], P('dp', None, 'heads')
- layer_update_step: float32 [8, 512, 32768], P('dp', None, 'heads')
All inputs are finite; a program needn't handle non-finite values.
Results may differ from a plain program's by a relative error of at most 0.015.
Values may be sent and summed in bfloat16 or wider, within the bound.
No kernel may reach another device: no remote copies, remote signals or barrier semaphores. Data moves between devices by JAX's collectives and lax.ppermute only.
A program may use at most 64 MiB of HBM per device.

v0:
```python
import math

import jax
import jax.numpy as jnp
from jax import lax
from jax.experimental import pallas as pl
from jax.experimental.pallas import tpu as pltpu
from jax.sharding import Mesh
from jax.sharding import PartitionSpec as P


LATENT = 512
HEADS = 128
NOPE = 128
ROPE = 64
VDIM = 128
SEQ = 128
HD = 4
QW = NOPE + ROPE
KVW = NOPE + VDIM
COLS_HERE = HD * KVW
TILE = 128
NT = LATENT // TILE
PAIRS = [(a, b) for a in range(NT) for b in range(a, NT)]

DP = ("zl", "core")
YX = ("y", "x")
NDP = 8
NYX = 16
ROWS = SEQ // NYX

poly_first = 3.4445
poly_second = -4.775
poly_third = 2.0315
norm_epsilon = 1e-07
decay_rate = 0.95

F32 = jnp.float32
BF16 = jnp.bfloat16


def contract_last(a, b):
    return lax.dot_general(a, b, (((1,), (1,)), ((), ())), preferred_element_type=F32)


def contract_first(a, b):
    return lax.dot_general(a, b, (((0,), (0,)), ((), ())), preferred_element_type=F32)


def up_project(rows, weight):
    return jnp.dot(rows[:, :LATENT], weight, preferred_element_type=F32).astype(BF16)


def attend(rows, kv, tokens):
    scale = 1.0 / math.sqrt(QW)
    key_at = lax.broadcasted_iota(jnp.int32, (SEQ, SEQ), 0)
    query_at = lax.broadcasted_iota(jnp.int32, (SEQ, SEQ), 1)
    allowed = key_at <= query_at
    queries, cots, scores, grad_probs = [], [], [], []
    for k in range(len(tokens)):
        at = slice(k * SEQ, (k + 1) * SEQ)
        for h in range(HD):
            keys = kv[at, h * KVW : h * KVW + NOPE]
            values = kv[at, h * KVW + NOPE : (h + 1) * KVW]
            query = tokens[k][:, h * QW : (h + 1) * QW]
            cot = tokens[k][:, HD * QW + h * VDIM : HD * QW + (h + 1) * VDIM]
            queries.append(query[:, :NOPE])
            cots.append(cot)
            scores.append(contract_last(jnp.concatenate([keys, rows[at, LATENT:]], axis=1), query))
            grad_probs.append(contract_last(values, cot))
    low, grads = [], []
    for score, grad_prob in zip(scores, grad_probs):
        score = jnp.where(allowed, score * scale, -jnp.inf)
        expd = jnp.exp(score - jnp.max(score, axis=0, keepdims=True))
        probs = expd * (1.0 / jnp.sum(expd, axis=0, keepdims=True))
        delta = jnp.sum(probs * grad_prob, axis=0, keepdims=True)
        low.append(probs.astype(BF16))
        grads.append((probs * (grad_prob - delta) * scale).astype(BF16))
    out = []
    for query, cot, probs, grad in zip(queries, cots, low, grads):
        out.append(jnp.dot(grad, query, preferred_element_type=F32).astype(BF16))
        out.append(jnp.dot(probs, cot, preferred_element_type=F32).astype(BF16))
    wide = 2 * HD
    return jnp.concatenate([jnp.concatenate(out[k * wide : (k + 1) * wide], axis=1) for k in range(len(tokens))], axis=0)


IN_VMEM = pl.BlockSpec(memory_space=pltpu.VMEM)


def read_chunks(chunks, refs):
    out, at = [], 0
    for parts in chunks:
        got = [r[...] for r in refs[at : at + len(parts)]]
        at += len(parts)
        if len(parts) == 2:
            half = HD * QW // 2
            got = [jnp.concatenate([g[:, :half] for g in got] + [g[:, half:] for g in got], axis=1)]
        out.append(got[0])
    return out


def first_sequences(rows, weight, chunks):
    n = len(chunks)
    flat = [part for parts in chunks for part in parts]

    def kernel(rows_ref, weight_ref, *refs):
        here = rows_ref[:n].reshape(n * SEQ, LATENT + ROPE)
        refs[-1][...] = attend(here, up_project(here, weight_ref[...]), read_chunks(chunks, refs))

    return pl.pallas_call(
        kernel,
        in_specs=[IN_VMEM] * (2 + len(flat)),
        out_specs=IN_VMEM,
        out_shape=jax.ShapeDtypeStruct((n * SEQ, COLS_HERE), BF16),
        name="first_sequences",
    )(rows, weight, *flat)


def middle_sequences(rows, weight, before, momentum, chunks):
    first, n = before.shape[0] // SEQ, len(chunks)
    flat = [part for parts in chunks for part in parts]

    def kernel(rows_ref, weight_ref, before_ref, mom_ref, *refs):
        sofar_ref, kv_ref = refs[-2], refs[-1]
        here = rows_ref[first:].reshape((n + 1) * SEQ, LATENT + ROPE)
        kv = up_project(here, weight_ref[...])
        kv_ref[...] = kv[n * SEQ :]
        dkv = jnp.concatenate([before_ref[...], attend(here, kv, read_chunks(chunks, refs))], axis=0)
        lat = rows_ref[: first + n].reshape((first + n) * SEQ, LATENT + ROPE)[:, :LATENT]
        sofar_ref[...] = decay_rate * mom_ref[...].astype(F32) + contract_first(lat, dkv)

    return pl.pallas_call(
        kernel,
        in_specs=[IN_VMEM] * (4 + len(flat)),
        out_specs=(IN_VMEM, IN_VMEM),
        out_shape=(
            jax.ShapeDtypeStruct((LATENT, COLS_HERE), F32),
            jax.ShapeDtypeStruct((SEQ, COLS_HERE), BF16),
        ),
        name="middle_sequences",
    )(rows, weight, before, momentum, *flat)


def last_sequence(rows, kv, sofar, chunk):
    half = LATENT // 2
    split_at = NT // 2

    def kernel(rows_hbm, kv_ref, chunk_ref, sofar_hbm, fresh_ref, gram_ref, rows_ref, sofar_ref, sems):
        load = pltpu.make_async_copy(sofar_hbm, sofar_ref, sems.at[0])
        load.start()
        load_rows = pltpu.make_async_copy(rows_hbm.at[NDP - 1], rows_ref, sems.at[1])
        load_rows.start()
        load_rows.wait()
        rows = rows_ref[...]
        dkv = attend(rows, kv_ref[...], [chunk_ref[...]])
        add = contract_first(rows[:, :LATENT], dkv)
        load.wait()
        fresh = (sofar_ref[...] + add).astype(BF16)
        fresh_ref[...] = fresh
        top = contract_last(fresh[:half], fresh).astype(BF16)
        low = contract_last(fresh[half:], fresh[half:]).astype(BF16)
        for k, (a, b) in enumerate(PAIRS):
            if a < split_at:
                gram_ref[k] = top[a * TILE : (a + 1) * TILE, b * TILE : (b + 1) * TILE]
            else:
                a, b = a - split_at, b - split_at
                gram_ref[k] = low[a * TILE : (a + 1) * TILE, b * TILE : (b + 1) * TILE]

    return pl.pallas_call(
        kernel,
        in_specs=[pl.BlockSpec(memory_space=pl.ANY), IN_VMEM, IN_VMEM, pl.BlockSpec(memory_space=pl.ANY)],
        out_specs=(IN_VMEM, IN_VMEM),
        out_shape=(
            jax.ShapeDtypeStruct((LATENT, COLS_HERE), BF16),
            jax.ShapeDtypeStruct((len(PAIRS), TILE, TILE), BF16),
        ),
        scratch_shapes=[
            pltpu.VMEM((SEQ, LATENT + ROPE), BF16),
            pltpu.VMEM((LATENT, COLS_HERE), F32),
            pltpu.SemaphoreType.DMA((2,)),
        ],
        name="last_sequence",
    )(rows, kv, chunk, sofar)


def split(a):
    high = a.astype(BF16)
    return high, (a - high.astype(F32)).astype(BF16)


def product(a, b):
    d = lambda u, v: jnp.dot(u, v, preferred_element_type=F32)
    return d(a[0], b[0]) + (d(a[0], b[1]) + d(a[1], b[0]))


def to_unit(t):
    p = jnp.ones_like(t)
    for e in (64, 32, 16, 8, 4, 2, 1):
        big = t >= 2.0**e
        t = jnp.where(big, t * 2.0**-e, t)
        p = jnp.where(big, p * 2.0**-e, p)
    for e in (64, 32, 16, 8, 4, 2, 1):
        small = t < 2.0 ** (1 - e)
        t = jnp.where(small, t * 2.0**e, t)
        p = jnp.where(small, p * 2.0**e, p)
    return t, p


def dot(a, b):
    return jnp.dot(a, b, preferred_element_type=F32)


def update(gram, fresh):
    width = COLS_HERE // 2
    update_scale = 0.2 * math.sqrt(max(LATENT, HEADS * KVW))

    def kernel(gram_ref, fresh_ref, out_ref, base_ref, high_ref, low_ref, factor_ref):
        @pl.when(pl.program_id(0) == 0)
        def _():
            on_diagonal = lax.broadcasted_iota(jnp.int32, (TILE, TILE), 0) == lax.broadcasted_iota(
                jnp.int32, (TILE, TILE), 1
            )
            squares = jnp.zeros((TILE, TILE), F32)
            for k, (a, b) in enumerate(PAIRS):
                if a == b:
                    squares = squares + jnp.where(on_diagonal, gram_ref[k].astype(F32), 0.0)
            squares = jnp.sum(jnp.sum(squares, axis=0, keepdims=True), axis=1, keepdims=True)
            norm = jnp.sqrt(squares) + norm_epsilon
            factor_ref[...] = jnp.broadcast_to(update_scale / norm, factor_ref.shape)
            ratio, power = to_unit(norm * norm)
            for k, (a, b) in enumerate(PAIRS):
                block = gram_ref[k].astype(F32) * power
                base_ref[a * TILE : (a + 1) * TILE, b * TILE : (b + 1) * TILE] = block.astype(BF16)
                if a != b:
                    base_ref[b * TILE : (b + 1) * TILE, a * TILE : (a + 1) * TILE] = block.T.astype(BF16)
            inv = 1.0 / ratio
            first = jnp.where(
                lax.broadcasted_iota(jnp.int32, (LATENT, LATENT), 0)
                == lax.broadcasted_iota(jnp.int32, (LATENT, LATENT), 1),
                poly_first,
                0.0,
            ).astype(F32)
            base = base_ref[...]
            poly = split(first + (poly_second * inv) * base.astype(F32) + (poly_third * inv * inv) * dot(base, base))
            square = split(product(poly, poly))
            inner = inv * (dot(base, square[0]) + dot(base, square[1]))
            inner2 = split(inner)
            later = first + poly_second * inner + poly_third * product(inner2, inner2)
            high, low = split(product(split(later), poly))
            high_ref[...] = high
            low_ref[...] = low

        fresh = fresh_ref[...]
        out_ref[...] = (dot(high_ref[...], fresh) + dot(low_ref[...], fresh)) * factor_ref[0:1, 0:1]

    return pl.pallas_call(
        kernel,
        grid=(COLS_HERE // width,),
        in_specs=[
            pl.BlockSpec((len(PAIRS), TILE, TILE), lambda t: (0, 0, 0)),
            pl.BlockSpec((LATENT, width), lambda t: (0, t)),
        ],
        out_specs=pl.BlockSpec((LATENT, width), lambda t: (0, t)),
        out_shape=jax.ShapeDtypeStruct((LATENT, COLS_HERE), F32),
        scratch_shapes=[
            pltpu.VMEM((LATENT, LATENT), BF16),
            pltpu.VMEM((LATENT, LATENT), BF16),
            pltpu.VMEM((LATENT, LATENT), BF16),
            pltpu.VMEM((8, TILE), F32),
        ],
        name="update",
    )(gram, fresh)


def reduce_gram(gram):
    pieces = gram.reshape(NYX, -1, TILE)
    got = lax.all_to_all(pieces, YX, 0, 0, tiled=True)
    mine = jnp.sum(got.astype(F32), axis=0).astype(BF16)
    other = lax.ppermute(mine, "zh", [(0, 1), (1, 0)])
    mine = (mine.astype(F32) + other.astype(F32)).astype(BF16)
    full = lax.all_to_all(jnp.broadcast_to(mine[None], pieces.shape), YX, 0, 0, tiled=True)
    return full.reshape(gram.shape)


def pick(a, index):
    return lax.dynamic_index_in_dim(a, index, 0, keepdims=False)


STEPS_FIRST = (0, 6, 7, 2)
STEPS_MIDDLE = (1, 3, 4)
STEP_LAST = 5
STEP_OPENING = 6
ORDER = STEPS_FIRST + STEPS_MIDDLE + (STEP_LAST,)
HALF_Q = HD * QW // 2
HALF_V = HD * VDIM // 2


def pack(queries, grad_out, cuts):
    widths = [(q.stop - q.start, v.stop - v.start) for _, q, v in cuts]

    def kernel(queries_ref, grads_ref, *refs):
        n = len(cuts)
        here = lax.axis_index(DP)
        copies = []
        for k, (s, q, v) in enumerate(cuts):
            wide = widths[k][0]
            copies.append(
                pltpu.make_async_copy(
                    queries_ref.at[here ^ s, :, q], refs[k].at[:, :wide], refs[n].at[2 * k]
                )
            )
            copies.append(
                pltpu.make_async_copy(
                    grads_ref.at[here ^ s, :, v], refs[k].at[:, wide:], refs[n].at[2 * k + 1]
                )
            )
        for copy in copies:
            copy.start()
        for copy in copies:
            copy.wait()

    anywhere = pl.BlockSpec(memory_space=pl.ANY)
    return pl.pallas_call(
        kernel,
        in_specs=[anywhere, anywhere],
        out_specs=[IN_VMEM] * len(cuts),
        out_shape=[jax.ShapeDtypeStruct((SEQ, a + b), BF16) for a, b in widths],
        scratch_shapes=[pltpu.SemaphoreType.DMA((2 * len(cuts),))],
    )(queries, grad_out)


def send(chunk, s):
    return lax.ppermute(chunk, DP, [(k, k ^ s) for k in range(NDP)])


def inner_body(latent, rope_keys, queries, grad_out, key_value_up_weight, momentum):
    here = lax.axis_index(DP)
    halves = pack(
        queries,
        grad_out,
        [(STEP_OPENING, slice(k * HALF_Q, (k + 1) * HALF_Q), slice(k * HALF_V, (k + 1) * HALF_V)) for k in range(2)],
    )
    halves, queries, grad_out, latent, rope_keys = lax.optimization_barrier(
        (halves, queries, grad_out, latent, rope_keys)
    )
    others = [s for s in ORDER if s != STEP_OPENING]
    packed = pack(queries, grad_out, [(s, slice(0, HD * QW), slice(0, HD * VDIM)) for s in others])
    chunks = {s: (send(chunk, s) if s else chunk,) for s, chunk in zip(others, packed)}
    chunks[STEP_OPENING] = tuple(send(h, STEP_OPENING) for h in halves)
    at = ROWS * lax.axis_index(YX)
    rows = jnp.concatenate(
        [lax.dynamic_slice_in_dim(latent, at, ROWS, axis=1), lax.dynamic_slice_in_dim(rope_keys, at, ROWS, axis=1)],
        axis=2,
    )
    rows = lax.all_to_all(rows, DP, 0, 0, tiled=True)
    rows = jnp.stack([pick(rows, here ^ s) for s in ORDER])
    rows = lax.all_to_all(jnp.broadcast_to(rows[None], (NYX,) + rows.shape), YX, 0, 0, tiled=True)
    rows = rows.transpose(1, 0, 2, 3).reshape(NDP, SEQ, LATENT + ROPE)

    weight = key_value_up_weight[0]
    dkv = first_sequences(rows, weight, [chunks[s] for s in STEPS_FIRST])
    sofar, kv = middle_sequences(rows, weight, dkv, momentum[0], [chunks[s] for s in STEPS_MIDDLE])
    fresh, gram = last_sequence(rows, kv, sofar, chunks[STEP_LAST][0])
    step = update(reduce_gram(gram), fresh)
    return fresh[None], step[None]


def solution(mesh):
    fine = Mesh(mesh.devices.reshape(4, 2, 4, 4, 2), ("zl", "core", "y", "x", "zh"))
    heads = ("y", "x", "zh")
    placed = (
        P(None, DP, None),
        P(None, DP, None),
        P(None, DP, heads),
        P(None, DP, heads),
        P(DP, None, heads),
        P(DP, None, heads),
    )
    return jax.shard_map(
        inner_body,
        mesh=fine,
        in_specs=placed,
        out_specs=(P(DP, None, heads), P(DP, None, heads)),
        check_vma=False,
    )
```

profile of v0, /device:TPU:32, one launch (start us, length us, event | category | flops | bytes accessed | tf_op | source)
XLA Modules:
  0.0 135.0 jit_solution(4654224759798164271)
XLA Ops:
  0.7 1.8 %shard_map.77 = (bf16[128,640]{1,0:T(8,128)(2,1)}, bf16[128,640]{1,0:T(8,128)(2,1)}) custom-call(bf16[8,128,768]{2,1,0:T(8,128)(2,1)} %queries_ref.2, bf16[8,128,512]{2,1,0:T(8,128)(2,1)} %grads_ref.2), custom_call_target="tpu_custom_call" | custom-call | tf_op jit(solution)/shard_map/pallas_call | solution.py:323
  2.8 0.7 pad_maximum_fusion
  3.4 6.0 %all-to-all-start = ((bf16[8,8,576]{2,1,0:T(8,128)(2,1)}), bf16[8,8,576]{2,1,0:T(8,128)(2,1)S(1)}, u32[]{:S(2)}, u32[]{:S(2)}) async-start(bf16[8,8,576]{2,1,0:T(8,128)(2,1)} %pad_maximum_fusion), calls=%async_computation | async-start | bytes 163840 | tf_op jit(solution)/shard_map/all_to_all | solution.py:355
  9.4 4.9 %all-to-all-done = bf16[8,8,576]{2,1,0:T(8,128)(2,1)S(1)} async-done(((bf16[8,8,576]{2,1,0:T(8,128)(2,1)}), bf16[8,8,576]{2,1,0:T(8,128)(2,1)S(1)}, u32[]{:S(2)}, u32[]{:S(2)}) %all-to-all-start) | async-done | bytes 73760 | tf_op jit(solution)/shard_map/all_to_all | solution.py:355
  14.4 1.2 broadcast_in_dim.8
  15.6 7.0 %all-to-all-start.1 = ((bf16[16,8,8,576]{3,2,1,0:T(8,128)(2,1)}), bf16[16,8,8,576]{3,2,1,0:T(8,128)(2,1)S(1)}, u32[]{:S(2)}, u32[]{:S(2)}) async-start(bf16[16,8,8,576]{3,2,1,0:T(8,128)(2,1)} %broadcast_in_dim.8), calls=%async_computation.1 | async-start | bytes 2621440 | tf_op jit(solution)/shard_map/all_to_all | solution.py:357
  22.6 3.2 %shard_map.78 = (bf16[128,1280]{1,0:T(8,128)(2,1)}, bf16[128,1280]{1,0:T(8,128)(2,1)}, bf16[128,1280]{1,0:T(8,128)(2,1)}, bf16[128,1280]{1,0:T(8,128)(2,1)}, bf1...) custom-call(bf16[8,128,768]{2,1,0:T(8,128)(2,1)} %queries_ref.2, ...), custom_call_target="tpu_custom_call" | custom-call | tf_op jit(solution)/shard_map/pallas_call | solution.py:323
  25.9 1.0 collective-permute-start
  27.0 1.1 collective-permute-start.1
  28.0 3.0 %collective-permute-start.3 = (bf16[128,1280]{1,0:T(8,128)(2,1)}, bf16[128,1280]{1,0:T(8,128)(2,1)S(1)}, u32[]{:S(2)}, u32[]{:S(2)}) collective-permute-start(bf16[128,1280]{1,0:T(8,128)(2,1)} %get-tuple-element.31), channel_id=1, source_target_pairs={{0,64},{32,96},{64,0},{96,32},{128,192},{160,224},{192,128},{224,1... | collective-permute-start | bytes 983048 | tf_op jit(solution)/shard_map/ppermute | solution.py:333
  31.3 21.6 %collective-permute-done.refs_1_ = bf16[128,640]{1,0:T(8,128)(2,1)S(1)} collective-permute-done((bf16[128,640]{1,0:T(8,128)(2,1)}, bf16[128,640]{1,0:T(8,128)(2,1)S(1)}, u32[]{:S(2)}, u32[]{:S(2)}) %collective-permute-start) | collective-permute-done | bytes 163872 | tf_op jit(solution)/shard_map/ppermute | solution.py:333
  52.9 3.5 %collective-permute-done.1.refs_2_ = bf16[128,640]{1,0:T(8,128)(2,1)S(1)} collective-permute-done((bf16[128,640]{1,0:T(8,128)(2,1)}, bf16[128,640]{1,0:T(8,128)(2,1)S(1)}, u32[]{:S(2)}, u32[]{:S(2)}) %collective-permute-start.1) | collective-permute-done | bytes 163872 | tf_op jit(solution)/shard_map/ppermute | solution.py:333
  57.1 2.3 %collective-permute-start.7 = (bf16[128,1280]{1,0:T(8,128)(2,1)}, bf16[128,1280]{1,0:T(8,128)(2,1)}, u32[]{:S(2)}, u32[]{:S(2)}) collective-permute-start(bf16[128,1280]{1,0:T(8,128)(2,1)} %get-tuple-element.36), channel_id=1, source_target_pairs={{0,160},{32,128},{64,224},{96,192},{128,32},{160,0},{192,96},{224,... | collective-permute-start | bytes 983048 | tf_op jit(solution)/shard_map/ppermute | solution.py:333
  59.4 1.2 copy_bitcast_fusion.rows_ref.rows_hbm
  60.6 0.7 copy-done.2
  61.3 4.6 %first_sequences.1.before_ref = bf16[512,1024]{1,0:T(8,128)(2,1)} custom-call(bf16[8,128,576]{2,1,0:T(8,128)(2,1)} %copy_bitcast_fusion.rows_ref.rows_hbm, bf16[512,1024]{1,0:T(8,128)(2,1)} %bitcast.11, bf16[128,1280]{1,0:T(8,128)(2,1)} %get-tuple-element.27.refs_0_, bf16[128,640]{1,0:T(8,128)(2,1)} %copy-done.4, bf16[128,640]{1,0:T(8,128)(2,1)} %copy-done.5, ...), custom_call_target="tpu_custom_call" | custom-call | tf_op jit(solution)/shard_map/first_sequences/pallas_call | solution.py:110
  66.5 12.5 %collective-permute-done.6.refs_2_ = bf16[128,1280]{1,0:T(8,128)(2,1)} collective-permute-done((bf16[128,1280]{1,0:T(8,128)(2,1)}, bf16[128,1280]{1,0:T(8,128)(2,1)}, u32[]{:S(2)}, u32[]{:S(2)}) %collective-permute-start.6) | collective-permute-done | bytes 327712 | tf_op jit(solution)/shard_map/ppermute | solution.py:333
  78.9 6.4 %middle_sequences.1 = (f32[512,1024]{1,0:T(8,128)}, bf16[128,1024]{1,0:T(8,128)(2,1)}) custom-call(bf16[8,128,576]{2,1,0:T(8,128)(2,1)} %copy_bitcast_fusion.rows_ref.rows_hbm, bf16[512,1024]{1,0:T(8,128)(2,1)} %bitcast.12, bf16[512,1024]{1,0:T(8,128)(2,1)} %first_sequences.1.before_ref, bf16[512,1024]{1,0:T(8,128)(2,1)} %bitcast.16, ...), custom_call_target="tpu_custom_call" | custom-call | tf_op jit(solution)/shard_map/middle_sequences/pallas_call | solution.py:132
  85.9 5.0 %last_sequence.1 = (bf16[512,1024]{1,0:T(8,128)(2,1)}, bf16[10,128,128]{2,1,0:T(8,128)(2,1)}) custom-call(bf16[8,128,576]{2,1,0:T(8,128)(2,1)} %copy_bitcast_fusion.rows_ref.rows_hbm, bf16[128,1024]{1,0:T(8,128)(2,1)} %get-tuple-element.35.kv_ref, bf16[128,1280]{1,0:T(8,128)(2,1)} %collective-permute-done.7.chunk_ref, f32[512,1024]{1,0:T(8,128)} %get-tuple-element.37.sofar_hbm), custom_call_target="tpu_custom_call" | custom-call | tf_op jit(solution)/shard_map/last_sequence/pallas_call | solution.py:169
  90.9 16.4 %all_to_all.20 = bf16[16,80,128]{2,1,0:T(8,128)(2,1)S(1)} all-to-all(bf16[16,80,128]{2,1,0:T(8,128)(2,1)} %bitcast.17), channel_id=1, replica_groups=mesh['zl'=4,'core'=2,'y'=4,'x'=4,'zh'=2] {'y','x'}, dimensions={0} | all-to-all | bytes 655360 | tf_op jit(solution)/shard_map/all_to_all | solution.py:277
  107.4 4.7 %collective-permute-start.8 = (bf16[80,128]{1,0:T(8,128)(2,1)S(1)}, bf16[80,128]{1,0:T(8,128)(2,1)S(1)}, u32[]{:S(2)}, u32[]{:S(2)}) collective-permute-start(bf16[80,128]{1,0:T(8,128)(2,1)S(1)} %reduce_sum.12), channel_id=1, source_target_pairs={{0,1},{1,0},{2,3},{3,2},{4,5},{5,4},{6,7},{7,6},{8,9},{9,8},{10,11... | collective-permute-start | bytes 61448 | tf_op jit(solution)/shard_map/ppermute | solution.py:279
  112.1 3.1 %collective-permute-done.8 = bf16[80,128]{1,0:T(8,128)(2,1)S(1)} collective-permute-done((bf16[80,128]{1,0:T(8,128)(2,1)S(1)}, bf16[80,128]{1,0:T(8,128)(2,1)S(1)}, u32[]{:S(2)}, u32[]{:S(2)}) %collective-permute-start.8) | collective-permute-done | bytes 20512 | tf_op jit(solution)/shard_map/ppermute | solution.py:279
  115.2 12.3 %all_to_all.21 = bf16[16,80,128]{2,1,0:T(8,128)(2,1)} all-to-all(bf16[16,80,128]{2,1,0:T(8,128)(2,1)S(1)} %broadcast_in_dim.20), channel_id=1, replica_groups=mesh['zl'=4,'core'=2,'y'=4,'x'=4,'zh'=2] {'y','x'}, dimensions={0} | all-to-all | bytes 655360 | tf_op jit(solution)/shard_map/all_to_all | solution.py:281
  127.6 7.4 %update.1 = f32[512,1024]{1,0:T(8,128)} custom-call(bf16[10,128,128]{2,1,0:T(8,128)(2,1)} %bitcast.14, bf16[512,1024]{1,0:T(8,128)(2,1)} %get-tuple-element.38.fresh_ref), custom_call_target="tpu_custom_call" | custom-call | tf_op jit(solution)/shard_map/update/pallas_call | solution.py:256
  (37 shorter events, 2.5 us)
Async XLA Ops:
  0.6 1.9 %copy-start = (bf16[8,128,512]{2,1,0:T(8,128)(2,1)S(1)}, bf16[8,128,512]{2,1,0:T(8,128)(2,1)}, u32[]{:S(2)}) copy-start(bf16[8,128,512]{2,1,0:T(8,128)(2,1)} %param.6) | copy-start | bytes 3145732
  0.7 1.9 %copy-start.6 = (bf16[8,128,64]{1,2,0:T(8,128)(2,1)S(1)}, bf16[8,128,64]{1,2,0:T(8,128)(2,1)}, u32[]{:S(2)}) copy-start(bf16[8,128,64]{1,2,0:T(8,128)(2,1)} %param.7) | copy-start | bytes 393220
  3.4 10.9 %all-to-all-start = ((bf16[8,8,576]{2,1,0:T(8,128)(2,1)}), bf16[8,8,576]{2,1,0:T(8,128)(2,1)S(1)}, u32[]{:S(2)}, u32[]{:S(2)}) async-start(bf16[8,8,576]{2,1,0:T(8,128)(2,1)} %pad_maximum_fusion), calls=%async_computation | async-start | bytes 163840 | tf_op jit(solution)/shard_map/all_to_all | solution.py:355
  15.6 43.8 %all-to-all-start.1 = ((bf16[16,8,8,576]{3,2,1,0:T(8,128)(2,1)}), bf16[16,8,8,576]{3,2,1,0:T(8,128)(2,1)S(1)}, u32[]{:S(2)}, u32[]{:S(2)}) async-start(bf16[16,8,8,576]{3,2,1,0:T(8,128)(2,1)} %broadcast_in_dim.8), calls=%async_computation.1 | async-start | bytes 2621440 | tf_op jit(solution)/shard_map/all_to_all | solution.py:357
  25.8 30.6 %collective-permute-start.2 = (bf16[128,1280]{1,0:T(8,128)(2,1)}, bf16[128,1280]{1,0:T(8,128)(2,1)S(1)}, u32[]{:S(2)}, u32[]{:S(2)}) collective-permute-start(bf16[128,1280]{1,0:T(8,128)(2,1)} %get-tuple-element.30), channel_id=1, source_target_pairs={{0,224},{32,192},{64,160},{96,128},{128,96},{160,64},{192,32},{224... | collective-permute-start | bytes 983048 | tf_op jit(solution)/shard_map/ppermute | solution.py:333
  25.9 27.0 %collective-permute-start = (bf16[128,640]{1,0:T(8,128)(2,1)}, bf16[128,640]{1,0:T(8,128)(2,1)S(1)}, u32[]{:S(2)}, u32[]{:S(2)}) collective-permute-start(bf16[128,640]{1,0:T(8,128)(2,1)} %get-tuple-element.28), channel_id=1, source_target_pairs={{0,192},{32,224},{64,128},{96,160},{128,64},{160,96},{192,0},{224,... | collective-permute-start | bytes 491528 | tf_op jit(solution)/shard_map/ppermute | solution.py:333
  27.0 29.4 %collective-permute-start.1 = (bf16[128,640]{1,0:T(8,128)(2,1)}, bf16[128,640]{1,0:T(8,128)(2,1)S(1)}, u32[]{:S(2)}, u32[]{:S(2)}) collective-permute-start(bf16[128,640]{1,0:T(8,128)(2,1)} %get-tuple-element.29), channel_id=1, source_target_pairs={{0,192},{32,224},{64,128},{96,160},{128,64},{160,96},{192,0},{224,... | collective-permute-start | bytes 491528 | tf_op jit(solution)/shard_map/ppermute | solution.py:333
  28.0 32.5 %collective-permute-start.3 = (bf16[128,1280]{1,0:T(8,128)(2,1)}, bf16[128,1280]{1,0:T(8,128)(2,1)S(1)}, u32[]{:S(2)}, u32[]{:S(2)}) collective-permute-start(bf16[128,1280]{1,0:T(8,128)(2,1)} %get-tuple-element.31), channel_id=1, source_target_pairs={{0,64},{32,96},{64,0},{96,32},{128,192},{160,224},{192,128},{224,1... | collective-permute-start | bytes 983048 | tf_op jit(solution)/shard_map/ppermute | solution.py:333
  31.1 34.9 %collective-permute-start.4 = (bf16[128,1280]{1,0:T(8,128)(2,1)}, bf16[128,1280]{1,0:T(8,128)(2,1)S(1)}, u32[]{:S(2)}, u32[]{:S(2)}) collective-permute-start(bf16[128,1280]{1,0:T(8,128)(2,1)} %get-tuple-element.32), channel_id=1, source_target_pairs={{0,32},{32,0},{64,96},{96,64},{128,160},{160,128},{192,224},{224,1... | collective-permute-start | bytes 983048 | tf_op jit(solution)/shard_map/ppermute | solution.py:333
  52.9 7.7 %copy-start.4 = (bf16[128,640]{1,0:T(8,128)(2,1)}, bf16[128,640]{1,0:T(8,128)(2,1)S(1)}, u32[]{:S(2)}) copy-start(bf16[128,640]{1,0:T(8,128)(2,1)S(1)} %collective-permute-done.refs_1_) | copy-start | bytes 491524
  52.9 13.5 %collective-permute-start.5 = (bf16[128,1280]{1,0:T(8,128)(2,1)}, bf16[128,1280]{1,0:T(8,128)(2,1)}, u32[]{:S(2)}, u32[]{:S(2)}) collective-permute-start(bf16[128,1280]{1,0:T(8,128)(2,1)} %get-tuple-element.33), channel_id=1, source_target_pairs={{0,96},{32,64},{64,32},{96,0},{128,224},{160,192},{192,160},{224,1... | collective-permute-start | bytes 983048 | tf_op jit(solution)/shard_map/ppermute | solution.py:333
  56.4 0.7 copy-start.5
  56.4 22.5 %collective-permute-start.6 = (bf16[128,1280]{1,0:T(8,128)(2,1)}, bf16[128,1280]{1,0:T(8,128)(2,1)}, u32[]{:S(2)}, u32[]{:S(2)}) collective-permute-start(bf16[128,1280]{1,0:T(8,128)(2,1)} %get-tuple-element.34), channel_id=1, source_target_pairs={{0,128},{32,160},{64,192},{96,224},{128,0},{160,32},{192,64},{224,... | collective-permute-start | bytes 983048 | tf_op jit(solution)/shard_map/ppermute | solution.py:333
  56.4 4.2 %copy-start.1 = (bf16[128,1280]{1,0:T(8,128)(2,1)}, bf16[128,1280]{1,0:T(8,128)(2,1)S(1)}, u32[]{:S(2)}) copy-start(bf16[128,1280]{1,0:T(8,128)(2,1)S(1)} %collective-permute-done.2.refs_3_) | copy-start | bytes 983044
  57.1 28.8 %collective-permute-start.7 = (bf16[128,1280]{1,0:T(8,128)(2,1)}, bf16[128,1280]{1,0:T(8,128)(2,1)}, u32[]{:S(2)}, u32[]{:S(2)}) collective-permute-start(bf16[128,1280]{1,0:T(8,128)(2,1)} %get-tuple-element.36), channel_id=1, source_target_pairs={{0,160},{32,128},{64,224},{96,192},{128,32},{160,0},{192,96},{224,... | collective-permute-start | bytes 983048 | tf_op jit(solution)/shard_map/ppermute | solution.py:333
  60.6 0.7 copy-start.2
  66.0 13.0 %copy-start.3 = (bf16[128,1280]{1,0:T(8,128)(2,1)}, bf16[128,1280]{1,0:T(8,128)(2,1)S(1)}, u32[]{:S(2)}) copy-start(bf16[128,1280]{1,0:T(8,128)(2,1)S(1)} %collective-permute-done.4.refs_0_) | copy-start | bytes 983044
  107.4 7.8 %collective-permute-start.8 = (bf16[80,128]{1,0:T(8,128)(2,1)S(1)}, bf16[80,128]{1,0:T(8,128)(2,1)S(1)}, u32[]{:S(2)}, u32[]{:S(2)}) collective-permute-start(bf16[80,128]{1,0:T(8,128)(2,1)S(1)} %reduce_sum.12), channel_id=1, source_target_pairs={{0,1},{1,0},{2,3},{3,2},{4,5},{5,4},{6,7},{7,6},{8,9},{9,8},{10,11... | collective-permute-start | bytes 61448 | tf_op jit(solution)/shard_map/ppermute | solution.py:279
where the time goes:
time: 137 us; the launch traced here: 135 us
  waiting for transfers between devices  46.6 us (34%)
  blocking collectives  28.7 us (21%)
  Pallas kernels  28.5 us (21%)
  starting transfers between devices  25.5 us (19%)
  local copies, waits for them, and re-layouts  4.15 us (3%)
    ppermute x8, waiting for transfers between devices, send(): return lax.ppermute(chunk, DP, [(k, k ^ s) for k in range(NDP)])  38.6 us
    all_to_all x1, blocking collectives, reduce_gram(): got = lax.all_to_all(pieces, YX, 0, 0, tiled=True)  16.4 us
    all_to_all x1, blocking collectives, reduce_gram(): lax.all_to_all(jnp.broadcast_to(mine[None], pieces.shape), YX, 0, 0, tile...  12.3 us
    ppermute x8, starting transfers between devices, send(): return lax.ppermute(chunk, DP, [(k, k ^ s) for k in range(NDP)])  7.77 us
    pallas_call x1, Pallas kernels, update(): pl.pallas_call(kernel, grid=(COLS_HERE // width,), in_specs=[pl.BlockSpec...  7.44 us
    all_to_all x1, starting transfers between devices, inner_body(): lax.all_to_all(jnp.broadcast_to(rows[None], (NYX,) + rows.shape), YX, 0,...  7.03 us
    pallas_call x1, Pallas kernels, middle_sequences(): pl.pallas_call(kernel, in_specs=[IN_VMEM] * (4 + len(flat)), out_specs=(I...  6.4 us
    all_to_all x1, starting transfers between devices, inner_body(): rows = lax.all_to_all(rows, DP, 0, 0, tiled=True)  6.01 us
  transfers between devices with their start and end apart: 11, of which 7 were waited for; matrix products, arithmetic and copies ran while one was open for 1% of the time, Pallas kernels for 11%

commit v1 on v0

--- a/solution.py
+++ b/solution.py
@@ -37,6 +37,7 @@
 
 F32 = jnp.float32
 BF16 = jnp.bfloat16
+VMEM_LIMIT = 65000 * 1024
 
 
 def contract_last(a, b):
@@ -99,64 +100,72 @@
     return out
 
 
-def first_sequences(rows, weight, chunks):
+ROOMY = pltpu.CompilerParams(vmem_limit_bytes=VMEM_LIMIT)
+
+
+def first_sequences(rows, weight, momentum, chunks):
     n = len(chunks)
     flat = [part for parts in chunks for part in parts]
 
-    def kernel(rows_ref, weight_ref, *refs):
+    def kernel(rows_ref, weight_ref, mom_ref, *refs):
         here = rows_ref[:n].reshape(n * SEQ, LATENT + ROPE)
-        refs[-1][...] = attend(here, up_project(here, weight_ref[...]), read_chunks(chunks, refs))
-
-    return pl.pallas_call(
-        kernel,
-        in_specs=[IN_VMEM] * (2 + len(flat)),
+        dkv = attend(here, up_project(here, weight_ref[...]), read_chunks(chunks, refs))
+        refs[-1][...] = decay_rate * mom_ref[...].astype(F32) + contract_first(here[:, :LATENT], dkv)
+
+    return pl.pallas_call(
+        kernel,
+        in_specs=[IN_VMEM] * (3 + len(flat)),
         out_specs=IN_VMEM,
-        out_shape=jax.ShapeDtypeStruct((n * SEQ, COLS_HERE), BF16),
+        out_shape=jax.ShapeDtypeStruct((LATENT, COLS_HERE), F32),
+        compiler_params=ROOMY,
         name="first_sequences",
-    )(rows, weight, *flat)
-
-
-def middle_sequences(rows, weight, before, momentum, chunks):
-    first, n = before.shape[0] // SEQ, len(chunks)
+    )(rows, weight, momentum, *flat)
+
+
+def middle_sequences(rows, weight, sofar, first, chunks):
+    n = len(chunks)
     flat = [part for parts in chunks for part in parts]
 
-    def kernel(rows_ref, weight_ref, before_ref, mom_ref, *refs):
-        sofar_ref, kv_ref = refs[-2], refs[-1]
+    def kernel(rows_ref, weight_ref, sofar_ref, *refs):
+        out_ref, kv_ref, last_ref, turned_ref = refs[-4:]
         here = rows_ref[first:].reshape((n + 1) * SEQ, LATENT + ROPE)
         kv = up_project(here, weight_ref[...])
         kv_ref[...] = kv[n * SEQ :]
-        dkv = jnp.concatenate([before_ref[...], attend(here, kv, read_chunks(chunks, refs))], axis=0)
-        lat = rows_ref[: first + n].reshape((first + n) * SEQ, LATENT + ROPE)[:, :LATENT]
-        sofar_ref[...] = decay_rate * mom_ref[...].astype(F32) + contract_first(lat, dkv)
-
-    return pl.pallas_call(
-        kernel,
-        in_specs=[IN_VMEM] * (4 + len(flat)),
-        out_specs=(IN_VMEM, IN_VMEM),
+        last = here[n * SEQ :]
+        last_ref[...] = last
+        turned_ref[...] = last[:, :LATENT].T
+        dkv = attend(here, kv, read_chunks(chunks, refs))
+        out_ref[...] = sofar_ref[...] + contract_first(here[: n * SEQ, :LATENT], dkv)
+
+    return pl.pallas_call(
+        kernel,
+        in_specs=[IN_VMEM] * (3 + len(flat)),
+        out_specs=(IN_VMEM,) * 4,
         out_shape=(
             jax.ShapeDtypeStruct((LATENT, COLS_HERE), F32),
             jax.ShapeDtypeStruct((SEQ, COLS_HERE), BF16),
+            jax.ShapeDtypeStruct((SEQ, LATENT + ROPE), BF16),
+            jax.ShapeDtypeStruct((LATENT, SEQ), BF16),
         ),
+        compiler_params=ROOMY,
         name="middle_sequences",
-    )(rows, weight, before, momentum, *flat)
-
-
-def last_sequence(rows, kv, sofar, chunk):
+    )(rows, weight, sofar, *flat)
+
+
+def last_sequence(rows, turned, kv, sofar, chunk):
     half = LATENT // 2
     split_at = NT // 2
 
-    def kernel(rows_hbm, kv_ref, chunk_ref, sofar_hbm, fresh_ref, gram_ref, rows_ref, sofar_ref, sems):
+    def kernel(rows_ref, turned_ref, kv_ref, chunk_ref, sofar_hbm, fresh_hbm, gram_ref, sofar_ref, fresh_ref, sems):
         load = pltpu.make_async_copy(sofar_hbm, sofar_ref, sems.at[0])
         load.start()
-        load_rows = pltpu.make_async_copy(rows_hbm.at[NDP - 1], rows_ref, sems.at[1])
-        load_rows.start()
-        load_rows.wait()
-        rows = rows_ref[...]
-        dkv = attend(rows, kv_ref[...], [chunk_ref[...]])
-        add = contract_first(rows[:, :LATENT], dkv)
+        dkv = attend(rows_ref[...], kv_ref[...], [chunk_ref[...]])
+        add = dot(turned_ref[...], dkv)
         load.wait()
         fresh = (sofar_ref[...] + add).astype(BF16)
         fresh_ref[...] = fresh
+        store = pltpu.make_async_copy(fresh_ref, fresh_hbm, sems.at[1])
+        store.start()
         top = contract_last(fresh[:half], fresh).astype(BF16)
         low = contract_last(fresh[half:], fresh[half:]).astype(BF16)
         for k, (a, b) in enumerate(PAIRS):
@@ -165,22 +174,24 @@
             else:
                 a, b = a - split_at, b - split_at
                 gram_ref[k] = low[a * TILE : (a + 1) * TILE, b * TILE : (b + 1) * TILE]
-
-    return pl.pallas_call(
-        kernel,
-        in_specs=[pl.BlockSpec(memory_space=pl.ANY), IN_VMEM, IN_VMEM, pl.BlockSpec(memory_space=pl.ANY)],
-        out_specs=(IN_VMEM, IN_VMEM),
+        store.wait()
+
+    anywhere = pl.BlockSpec(memory_space=pl.ANY)
+    return pl.pallas_call(
+        kernel,
+        in_specs=[IN_VMEM] * 4 + [anywhere],
+        out_specs=(anywhere, IN_VMEM),
         out_shape=(
             jax.ShapeDtypeStruct((LATENT, COLS_HERE), BF16),
             jax.ShapeDtypeStruct((len(PAIRS), TILE, TILE), BF16),
         ),
         scratch_shapes=[
-            pltpu.VMEM((SEQ, LATENT + ROPE), BF16),
             pltpu.VMEM((LATENT, COLS_HERE), F32),
+            pltpu.VMEM((LATENT, COLS_HERE), BF16),
             pltpu.SemaphoreType.DMA((2,)),
         ],
         name="last_sequence",
-    )(rows, kv, chunk, sofar)
+    )(rows, turned, kv, chunk, sofar)
 
 
 def split(a):
@@ -193,17 +204,11 @@
     return d(a[0], b[0]) + (d(a[0], b[1]) + d(a[1], b[0]))
 
 
-def to_unit(t):
-    p = jnp.ones_like(t)
-    for e in (64, 32, 16, 8, 4, 2, 1):
-        big = t >= 2.0**e
-        t = jnp.where(big, t * 2.0**-e, t)
-        p = jnp.where(big, p * 2.0**-e, p)
-    for e in (64, 32, 16, 8, 4, 2, 1):
-        small = t < 2.0 ** (1 - e)
-        t = jnp.where(small, t * 2.0**e, t)
-        p = jnp.where(small, p * 2.0**e, p)
-    return t, p
+def to_range(t):
+    p = jnp.full_like(t, 2.0**64)
+    for edge in (-48, -16, 16, 48, 80):
+        p = jnp.where(t >= 2.0**edge, 2.0 ** -(edge + 16), p)
+    return t * p, p
 
 
 def dot(a, b):
@@ -211,62 +216,64 @@
 
 
 def update(gram, fresh):
-    width = COLS_HERE // 2
     update_scale = 0.2 * math.sqrt(max(LATENT, HEADS * KVW))
-
-    def kernel(gram_ref, fresh_ref, out_ref, base_ref, high_ref, low_ref, factor_ref):
-        @pl.when(pl.program_id(0) == 0)
-        def _():
-            on_diagonal = lax.broadcasted_iota(jnp.int32, (TILE, TILE), 0) == lax.broadcasted_iota(
-                jnp.int32, (TILE, TILE), 1
-            )
-            squares = jnp.zeros((TILE, TILE), F32)
-            for k, (a, b) in enumerate(PAIRS):
-                if a == b:
-                    squares = squares + jnp.where(on_diagonal, gram_ref[k].astype(F32), 0.0)
-            squares = jnp.sum(jnp.sum(squares, axis=0, keepdims=True), axis=1, keepdims=True)
-            norm = jnp.sqrt(squares) + norm_epsilon
-            factor_ref[...] = jnp.broadcast_to(update_scale / norm, factor_ref.shape)
-            ratio, power = to_unit(norm * norm)
-            for k, (a, b) in enumerate(PAIRS):
-                block = gram_ref[k].astype(F32) * power
-                base_ref[a * TILE : (a + 1) * TILE, b * TILE : (b + 1) * TILE] = block.astype(BF16)
-                if a != b:
-                    base_ref[b * TILE : (b + 1) * TILE, a * TILE : (a + 1) * TILE] = block.T.astype(BF16)
-            inv = 1.0 / ratio
-            first = jnp.where(
-                lax.broadcasted_iota(jnp.int32, (LATENT, LATENT), 0)
-                == lax.broadcasted_iota(jnp.int32, (LATENT, LATENT), 1),
-                poly_first,
-                0.0,
-            ).astype(F32)
-            base = base_ref[...]
-            poly = split(first + (poly_second * inv) * base.astype(F32) + (poly_third * inv * inv) * dot(base, base))
-            square = split(product(poly, poly))
-            inner = inv * (dot(base, square[0]) + dot(base, square[1]))
-            inner2 = split(inner)
-            later = first + poly_second * inner + poly_third * product(inner2, inner2)
-            high, low = split(product(split(later), poly))
-            high_ref[...] = high
-            low_ref[...] = low
-
-        fresh = fresh_ref[...]
-        out_ref[...] = (dot(high_ref[...], fresh) + dot(low_ref[...], fresh)) * factor_ref[0:1, 0:1]
-
-    return pl.pallas_call(
-        kernel,
-        grid=(COLS_HERE // width,),
-        in_specs=[
-            pl.BlockSpec((len(PAIRS), TILE, TILE), lambda t: (0, 0, 0)),
-            pl.BlockSpec((LATENT, width), lambda t: (0, t)),
-        ],
-        out_specs=pl.BlockSpec((LATENT, width), lambda t: (0, t)),
+    parts = 4
+    width = COLS_HERE // parts
+
+    def kernel(gram_ref, fresh_hbm, out_hbm, fresh_ref, base_ref, out_ref, sems):
+        load = pltpu.make_async_copy(fresh_hbm, fresh_ref, sems.at[0])
+        load.start()
+        on_diagonal = lax.broadcasted_iota(jnp.int32, (TILE, TILE), 0) == lax.broadcasted_iota(
+            jnp.int32, (TILE, TILE), 1
+        )
+        squares = jnp.zeros((TILE, TILE), F32)
+        for k, (a, b) in enumerate(PAIRS):
+            if a == b:
+                squares = squares + jnp.where(on_diagonal, gram_ref[k].astype(F32), 0.0)
+        squares = jnp.sum(jnp.sum(squares, axis=0, keepdims=True), axis=1, keepdims=True)
+        norm = jnp.sqrt(squares) + norm_epsilon
+        ratio, power = to_range(norm * norm)
+        low_power = power.astype(BF16)
+        for k, (a, b) in enumerate(PAIRS):
+            block = gram_ref[k]
+            base_ref[a * TILE : (a + 1) * TILE, b * TILE : (b + 1) * TILE] = block * low_power
+            if a != b:
+                base_ref[b * TILE : (b + 1) * TILE, a * TILE : (a + 1) * TILE] = block.T * low_power
+        inv = 1.0 / ratio
+        first = jnp.where(
+            lax.broadcasted_iota(jnp.int32, (LATENT, LATENT), 0)
+            == lax.broadcasted_iota(jnp.int32, (LATENT, LATENT), 1),
+            poly_first,
+            0.0,
+        ).astype(F32)
+        base = base_ref[...]
+        poly = split(first + (poly_second * inv) * base.astype(F32) + (poly_third * inv * inv) * dot(base, base))
+        inner = (inv * dot(base, product(poly, poly).astype(BF16))).astype(BF16)
+        later = first + poly_second * inner.astype(F32) + poly_third * dot(inner, inner)
+        high, low = split(product(split(later), poly))
+        factor = update_scale / norm
+        load.wait()
+        stores = []
+        for k in range(parts):
+            at = slice(k * width, (k + 1) * width)
+            fresh = fresh_ref[:, at]
+            out_ref[:, at] = (dot(high, fresh) + dot(low, fresh)) * factor
+            stores.append(pltpu.make_async_copy(out_ref.at[:, at], out_hbm.at[:, at], sems.at[1 + k]))
+            stores[-1].start()
+        for store in stores:
+            store.wait()
+
+    anywhere = pl.BlockSpec(memory_space=pl.ANY)
+    return pl.pallas_call(
+        kernel,
+        in_specs=[IN_VMEM, anywhere],
+        out_specs=anywhere,
         out_shape=jax.ShapeDtypeStruct((LATENT, COLS_HERE), F32),
         scratch_shapes=[
+            pltpu.VMEM((LATENT, COLS_HERE), BF16),
             pltpu.VMEM((LATENT, LATENT), BF16),
-            pltpu.VMEM((LATENT, LATENT), BF16),
-            pltpu.VMEM((LATENT, LATENT), BF16),
-            pltpu.VMEM((8, TILE), F32),
+            pltpu.VMEM((LATENT, COLS_HERE), F32),
+            pltpu.SemaphoreType.DMA((1 + parts,)),
         ],
         name="update",
     )(gram, fresh)
@@ -286,8 +293,8 @@
     return lax.dynamic_index_in_dim(a, index, 0, keepdims=False)
 
 
-STEPS_FIRST = (0, 6, 7, 2)
-STEPS_MIDDLE = (1, 3, 4)
+STEPS_FIRST = (0, 6, 7, 1, 2)
+STEPS_MIDDLE = (3, 4)
 STEP_LAST = 5
 STEP_OPENING = 6
 ORDER = STEPS_FIRST + STEPS_MIDDLE + (STEP_LAST,)
@@ -358,9 +365,11 @@
     rows = rows.transpose(1, 0, 2, 3).reshape(NDP, SEQ, LATENT + ROPE)
 
     weight = key_value_up_weight[0]
-    dkv = first_sequences(rows, weight, [chunks[s] for s in STEPS_FIRST])
-    sofar, kv = middle_sequences(rows, weight, dkv, momentum[0], [chunks[s] for s in STEPS_MIDDLE])
-    fresh, gram = last_sequence(rows, kv, sofar, chunks[STEP_LAST][0])
+    sofar = first_sequences(rows, weight, momentum[0], [chunks[s] for s in STEPS_FIRST])
+    sofar, kv, last_rows, turned = middle_sequences(
+        rows, weight, sofar, len(STEPS_FIRST), [chunks[s] for s in STEPS_MIDDLE]
+    )
+    fresh, gram = last_sequence(last_rows, turned, kv, sofar, chunks[STEP_LAST][0])
     step = update(reduce_gram(gram), fresh)
     return fresh[None], step[None]
 

time: 137 us -> 137 us (level)
  waiting for transfers between devices: 46.6 us -> 44.8 us
    ppermute x8, waiting for transfers between devices: 38.6 us -> 36.9 us  [send(): return lax.ppermute(chunk, DP, [(k, k ^ s) for k in range(NDP)])]
  transfers between devices with their start and end apart: 11 -> 11, of which waited for: 7 -> 6; matrix products, arithmetic and copies ran while one was open for 1% -> 1% of each run, Pallas kernels for 11% -> 11%
where the time goes in v1:
time: 137 us; the launch traced here: 135 us
  waiting for transfers between devices  44.8 us (33%)
  blocking collectives  28.7 us (21%)
  Pallas kernels  28.1 us (21%)
  starting transfers between devices  26.3 us (19%)
  local copies, waits for them, and re-layouts  5.09 us (4%)
    ppermute x8, waiting for transfers between devices, send(): return lax.ppermute(chunk, DP, [(k, k ^ s) for k in range(NDP)])  36.9 us
    all_to_all x1, blocking collectives, reduce_gram(): got = lax.all_to_all(pieces, YX, 0, 0, tiled=True)  16.4 us
    all_to_all x1, blocking collectives, reduce_gram(): lax.all_to_all(jnp.broadcast_to(mine[None], pieces.shape), YX, 0, 0, tile...  12.3 us
    ppermute x8, starting transfers between devices, send(): return lax.ppermute(chunk, DP, [(k, k ^ s) for k in range(NDP)])  8.6 us
    all_to_all x1, starting transfers between devices, inner_body(): lax.all_to_all(jnp.broadcast_to(rows[None], (NYX,) + rows.shape), YX, 0,...  7.03 us
    pallas_call x1, Pallas kernels, first_sequences(): pl.pallas_call(kernel, in_specs=[IN_VMEM] * (3 + len(flat)), out_specs=IN...  6.59 us
    pallas_call x1, Pallas kernels, update(): pl.pallas_call(kernel, in_specs=[IN_VMEM, anywhere], out_specs=anywhere,...  6.42 us
    all_to_all x1, starting transfers between devices, inner_body(): rows = lax.all_to_all(rows, DP, 0, 0, tiled=True)  6.01 us
  transfers between devices with their start and end apart: 11, of which 6 were waited for; matrix products, arithmetic and copies ran while one was open for 1% of the time, Pallas kernels for 11%

profile of v1, /device:TPU:32, one launch (start us, length us, event | category | flops | bytes accessed | tf_op | source)
XLA Modules:
  0.0 134.7 jit_solution(10843824376903448787)
XLA Ops:
  0.7 1.8 %shard_map.77 = (bf16[128,640]{1,0:T(8,128)(2,1)}, bf16[128,640]{1,0:T(8,128)(2,1)}) custom-call(bf16[8,128,768]{2,1,0:T(8,128)(2,1)} %queries_ref.2, bf16[8,128,512]{2,1,0:T(8,128)(2,1)} %grads_ref.2), custom_call_target="tpu_custom_call" | custom-call | tf_op jit(solution)/shard_map/pallas_call | solution.py:330
  2.5 0.9 constant_dynamic-slice_fusion.1
  4.2 6.0 %all-to-all-start = ((bf16[8,8,576]{2,1,0:T(8,128)(2,1)}), bf16[8,8,576]{2,1,0:T(8,128)(2,1)S(1)}, u32[]{:S(2)}, u32[]{:S(2)}) async-start(bf16[8,8,576]{2,1,0:T(8,128)(2,1)} %pad_maximum_fusion), calls=%async_computation | async-start | bytes 163840 | tf_op jit(solution)/shard_map/all_to_all | solution.py:362
  10.2 4.9 %all-to-all-done = bf16[8,8,576]{2,1,0:T(8,128)(2,1)S(1)} async-done(((bf16[8,8,576]{2,1,0:T(8,128)(2,1)}), bf16[8,8,576]{2,1,0:T(8,128)(2,1)S(1)}, u32[]{:S(2)}, u32[]{:S(2)}) %all-to-all-start) | async-done | bytes 73760 | tf_op jit(solution)/shard_map/all_to_all | solution.py:362
  15.1 1.2 broadcast_in_dim.8
  16.4 7.0 %all-to-all-start.1 = ((bf16[16,8,8,576]{3,2,1,0:T(8,128)(2,1)}), bf16[16,8,8,576]{3,2,1,0:T(8,128)(2,1)S(1)}, u32[]{:S(2)}, u32[]{:S(2)}) async-start(bf16[16,8,8,576]{3,2,1,0:T(8,128)(2,1)} %broadcast_in_dim.8), calls=%async_computation.1 | async-start | bytes 2621440 | tf_op jit(solution)/shard_map/all_to_all | solution.py:364
  23.4 3.2 %shard_map.78 = (bf16[128,1280]{1,0:T(8,128)(2,1)}, bf16[128,1280]{1,0:T(8,128)(2,1)}, bf16[128,1280]{1,0:T(8,128)(2,1)}, bf16[128,1280]{1,0:T(8,128)(2,1)}, bf1...) custom-call(bf16[8,128,768]{2,1,0:T(8,128)(2,1)} %queries_ref.2, ...), custom_call_target="tpu_custom_call" | custom-call | tf_op jit(solution)/shard_map/pallas_call | solution.py:330
  26.7 1.0 collective-permute-start
  27.8 1.1 collective-permute-start.1
  28.9 3.5 %collective-permute-start.4 = (bf16[128,1280]{1,0:T(8,128)(2,1)}, bf16[128,1280]{1,0:T(8,128)(2,1)S(1)}, u32[]{:S(2)}, u32[]{:S(2)}) collective-permute-start(bf16[128,1280]{1,0:T(8,128)(2,1)} %get-tuple-element.34), channel_id=1, source_target_pairs={{0,64},{32,96},{64,0},{96,32},{128,192},{160,224},{192,128},{224,1... | collective-permute-start | bytes 983048 | tf_op jit(solution)/shard_map/ppermute | solution.py:340
  32.4 21.3 %collective-permute-done.refs_1_ = bf16[128,640]{1,0:T(8,128)(2,1)S(1)} collective-permute-done((bf16[128,640]{1,0:T(8,128)(2,1)S(1)}, bf16[128,640]{1,0:T(8,128)(2,1)S(1)}, u32[]{:S(2)}, u32[]{:S(2)}) %collective-permute-start) | collective-permute-done | bytes 163872 | tf_op jit(solution)/shard_map/ppermute | solution.py:340
  53.7 3.5 %collective-permute-done.1.refs_2_ = bf16[128,640]{1,0:T(8,128)(2,1)S(1)} collective-permute-done((bf16[128,640]{1,0:T(8,128)(2,1)S(1)}, bf16[128,640]{1,0:T(8,128)(2,1)S(1)}, u32[]{:S(2)}, u32[]{:S(2)}) %collective-permute-start.1) | collective-permute-done | bytes 163872 | tf_op jit(solution)/shard_map/ppermute | solution.py:340
  57.3 2.8 %collective-permute-start.7 = (bf16[128,1280]{1,0:T(8,128)(2,1)}, bf16[128,1280]{1,0:T(8,128)(2,1)}, u32[]{:S(2)}, u32[]{:S(2)}) collective-permute-start(bf16[128,1280]{1,0:T(8,128)(2,1)} %get-tuple-element.40), channel_id=1, source_target_pairs={{0,160},{32,128},{64,224},{96,192},{128,32},{160,0},{192,96},{224,... | collective-permute-start | bytes 983048 | tf_op jit(solution)/shard_map/ppermute | solution.py:340
  60.1 1.2 copy_bitcast_fusion.rows_ref
  62.8 6.6 %first_sequences.1.sofar_ref = f32[512,1024]{1,0:T(8,128)} custom-call(bf16[8,128,576]{2,1,0:T(8,128)(2,1)} %copy_bitcast_fusion.rows_ref, bf16[512,1024]{1,0:T(8,128)(2,1)} %bitcast.11, bf16[512,1024]{1,0:T(8,128)(2,1)} %bitcast.15, bf16[128,1280]{1,0:T(8,128)(2,1)} %get-tuple-element.29.refs_0_, bf16[128,640]{1,0:T(8,128)(2,1)} %copy-done.4, ...), custom_call_target="tpu_custom_call" | custom-call | tf_op jit(solution)/shard_map/first_sequences/pallas_call | solution.py:115
  69.4 10.4 %collective-permute-done.6.refs_1_ = bf16[128,1280]{1,0:T(8,128)(2,1)} collective-permute-done((bf16[128,1280]{1,0:T(8,128)(2,1)}, bf16[128,1280]{1,0:T(8,128)(2,1)}, u32[]{:S(2)}, u32[]{:S(2)}) %collective-permute-start.6) | collective-permute-done | bytes 327712 | tf_op jit(solution)/shard_map/ppermute | solution.py:340
  79.7 5.3 %middle_sequences.1 = (f32[512,1024]{1,0:T(8,128)}, bf16[128,1024]{1,0:T(8,128)(2,1)}, bf16[128,576]{1,0:T(8,128)(2,1)}, bf16[512,128]{1,0:T(8,128)(2,1)}) custom-call(bf16[8,128,576]{2,1,0:T(8,128)(2,1)} %copy_bitcast_fusion.rows_ref, bf16[512,1024]{1,0:T(8,128)(2,1)} %bitcast.12, f32[512,1024]{1,0:T(8,128)} %first_sequences.1.sofar_ref, ...), custom_call_target="tpu_custom_call" | custom-call | tf_op jit(solution)/shard_map/middle_sequences/pallas_call | solution.py:140
  85.0 1.7 %collective-permute-done.7.chunk_ref = bf16[128,1280]{1,0:T(8,128)(2,1)} collective-permute-done((bf16[128,1280]{1,0:T(8,128)(2,1)}, bf16[128,1280]{1,0:T(8,128)(2,1)}, u32[]{:S(2)}, u32[]{:S(2)}) %collective-permute-start.7) | collective-permute-done | bytes 327712 | tf_op jit(solution)/shard_map/ppermute | solution.py:340
  86.7 4.8 %last_sequence.1 = (bf16[512,1024]{1,0:T(8,128)(2,1)}, bf16[10,128,128]{2,1,0:T(8,128)(2,1)}) custom-call(bf16[128,576]{1,0:T(8,128)(2,1)} %get-tuple-element.37.rows_ref, bf16[512,128]{1,0:T(8,128)(2,1)} %get-tuple-element.38.turned_ref, bf16[128,1024]{1,0:T(8,128)(2,1)} %get-tuple-element.39.kv_ref, bf16[128,1280]{1,0:T(8,128)(2,1)} %collective-permute-done.7.chunk_ref, ...), custom_call_target="tpu_custom_call" | custom-call | tf_op jit(solution)/shard_map/last_sequence/pallas_call | solution.py:180
  91.5 16.4 %all_to_all.20 = bf16[16,80,128]{2,1,0:T(8,128)(2,1)S(1)} all-to-all(bf16[16,80,128]{2,1,0:T(8,128)(2,1)} %bitcast.17), channel_id=1, replica_groups=mesh['zl'=4,'core'=2,'y'=4,'x'=4,'zh'=2] {'y','x'}, dimensions={0} | all-to-all | bytes 655360 | tf_op jit(solution)/shard_map/all_to_all | solution.py:284
  108.0 4.7 %collective-permute-start.8 = (bf16[80,128]{1,0:T(8,128)(2,1)S(1)}, bf16[80,128]{1,0:T(8,128)(2,1)S(1)}, u32[]{:S(2)}, u32[]{:S(2)}) collective-permute-start(bf16[80,128]{1,0:T(8,128)(2,1)S(1)} %reduce_sum.12), channel_id=1, source_target_pairs={{0,1},{1,0},{2,3},{3,2},{4,5},{5,4},{6,7},{7,6},{8,9},{9,8},{10,11... | collective-permute-start | bytes 61448 | tf_op jit(solution)/shard_map/ppermute | solution.py:286
  112.6 3.1 %collective-permute-done.8 = bf16[80,128]{1,0:T(8,128)(2,1)S(1)} collective-permute-done((bf16[80,128]{1,0:T(8,128)(2,1)S(1)}, bf16[80,128]{1,0:T(8,128)(2,1)S(1)}, u32[]{:S(2)}, u32[]{:S(2)}) %collective-permute-start.8) | collective-permute-done | bytes 20512 | tf_op jit(solution)/shard_map/ppermute | solution.py:286
  115.8 12.3 %all_to_all.21 = bf16[16,80,128]{2,1,0:T(8,128)(2,1)} all-to-all(bf16[16,80,128]{2,1,0:T(8,128)(2,1)S(1)} %broadcast_in_dim.20), channel_id=1, replica_groups=mesh['zl'=4,'core'=2,'y'=4,'x'=4,'zh'=2] {'y','x'}, dimensions={0} | all-to-all | bytes 655360 | tf_op jit(solution)/shard_map/all_to_all | solution.py:288
  128.1 6.4 %update.1 = f32[512,1024]{1,0:T(8,128)} custom-call(bf16[10,128,128]{2,1,0:T(8,128)(2,1)} %bitcast.14, bf16[512,1024]{1,0:T(8,128)(2,1)} %get-tuple-element.42.fresh_hbm), custom_call_target="tpu_custom_call" | custom-call | tf_op jit(solution)/shard_map/update/pallas_call | solution.py:267
  (39 shorter events, 2.7 us)
Async XLA Ops:
  0.6 2.7 %copy-start = (bf16[8,128,64]{1,2,0:T(8,128)(2,1)S(1)}, bf16[8,128,64]{1,2,0:T(8,128)(2,1)}, u32[]{:S(2)}) copy-start(bf16[8,128,64]{1,2,0:T(8,128)(2,1)} %param.7) | copy-start | bytes 393220
  4.2 10.9 %all-to-all-start = ((bf16[8,8,576]{2,1,0:T(8,128)(2,1)}), bf16[8,8,576]{2,1,0:T(8,128)(2,1)S(1)}, u32[]{:S(2)}, u32[]{:S(2)}) async-start(bf16[8,8,576]{2,1,0:T(8,128)(2,1)} %pad_maximum_fusion), calls=%async_computation | async-start | bytes 163840 | tf_op jit(solution)/shard_map/all_to_all | solution.py:362
  16.4 43.7 %all-to-all-start.1 = ((bf16[16,8,8,576]{3,2,1,0:T(8,128)(2,1)}), bf16[16,8,8,576]{3,2,1,0:T(8,128)(2,1)S(1)}, u32[]{:S(2)}, u32[]{:S(2)}) async-start(bf16[16,8,8,576]{3,2,1,0:T(8,128)(2,1)} %broadcast_in_dim.8), calls=%async_computation.1 | async-start | bytes 2621440 | tf_op jit(solution)/shard_map/all_to_all | solution.py:364
  23.4 3.3 %copy-start.7 = (bf16[128,640]{1,0:T(8,128)(2,1)S(1)}, bf16[128,640]{1,0:T(8,128)(2,1)}, u32[]{:S(2)}) copy-start(bf16[128,640]{1,0:T(8,128)(2,1)} %get-tuple-element.30) | copy-start | bytes 491524
  23.4 4.4 %copy-start.6 = (bf16[128,640]{1,0:T(8,128)(2,1)S(1)}, bf16[128,640]{1,0:T(8,128)(2,1)}, u32[]{:S(2)}) copy-start(bf16[128,640]{1,0:T(8,128)(2,1)} %get-tuple-element.31) | copy-start | bytes 491524
  26.6 30.6 %collective-permute-start.2 = (bf16[128,1280]{1,0:T(8,128)(2,1)}, bf16[128,1280]{1,0:T(8,128)(2,1)S(1)}, u32[]{:S(2)}, u32[]{:S(2)}) collective-permute-start(bf16[128,1280]{1,0:T(8,128)(2,1)} %get-tuple-element.32), channel_id=1, source_target_pairs={{0,224},{32,192},{64,160},{96,128},{128,96},{160,64},{192,32},{224... | collective-permute-start | bytes 983048 | tf_op jit(solution)/shard_map/ppermute | solution.py:340
  26.7 27.0 %collective-permute-start = (bf16[128,640]{1,0:T(8,128)(2,1)S(1)}, bf16[128,640]{1,0:T(8,128)(2,1)S(1)}, u32[]{:S(2)}, u32[]{:S(2)}) collective-permute-start(bf16[128,640]{1,0:T(8,128)(2,1)S(1)} %copy-done.7), channel_id=1, source_target_pairs={{0,192},{32,224},{64,128},{96,160},{128,64},{160,96},{192,0},{224,... | collective-permute-start | bytes 491528 | tf_op jit(solution)/shard_map/ppermute | solution.py:340
  27.8 29.4 %collective-permute-start.1 = (bf16[128,640]{1,0:T(8,128)(2,1)S(1)}, bf16[128,640]{1,0:T(8,128)(2,1)S(1)}, u32[]{:S(2)}, u32[]{:S(2)}) collective-permute-start(bf16[128,640]{1,0:T(8,128)(2,1)S(1)} %copy-done.6), channel_id=1, source_target_pairs={{0,192},{32,224},{64,128},{96,160},{128,64},{160,96},{192,0},{224,... | collective-permute-start | bytes 491528 | tf_op jit(solution)/shard_map/ppermute | solution.py:340
  28.9 32.5 %collective-permute-start.3 = (bf16[128,1280]{1,0:T(8,128)(2,1)}, bf16[128,1280]{1,0:T(8,128)(2,1)S(1)}, u32[]{:S(2)}, u32[]{:S(2)}) collective-permute-start(bf16[128,1280]{1,0:T(8,128)(2,1)} %get-tuple-element.33), channel_id=1, source_target_pairs={{0,32},{32,0},{64,96},{96,64},{128,160},{160,128},{192,224},{224,1... | collective-permute-start | bytes 983048 | tf_op jit(solution)/shard_map/ppermute | solution.py:340
  28.9 33.2 %collective-permute-start.4 = (bf16[128,1280]{1,0:T(8,128)(2,1)}, bf16[128,1280]{1,0:T(8,128)(2,1)S(1)}, u32[]{:S(2)}, u32[]{:S(2)}) collective-permute-start(bf16[128,1280]{1,0:T(8,128)(2,1)} %get-tuple-element.34), channel_id=1, source_target_pairs={{0,64},{32,96},{64,0},{96,32},{128,192},{160,224},{192,128},{224,1... | collective-permute-start | bytes 983048 | tf_op jit(solution)/shard_map/ppermute | solution.py:340
  53.7 7.6 %copy-start.4 = (bf16[128,640]{1,0:T(8,128)(2,1)}, bf16[128,640]{1,0:T(8,128)(2,1)S(1)}, u32[]{:S(2)}) copy-start(bf16[128,640]{1,0:T(8,128)(2,1)S(1)} %collective-permute-done.refs_1_) | copy-start | bytes 491524
  53.7 15.7 %collective-permute-start.5 = (bf16[128,1280]{1,0:T(8,128)(2,1)}, bf16[128,1280]{1,0:T(8,128)(2,1)}, u32[]{:S(2)}, u32[]{:S(2)}) collective-permute-start(bf16[128,1280]{1,0:T(8,128)(2,1)} %get-tuple-element.35), channel_id=1, source_target_pairs={{0,96},{32,64},{64,32},{96,0},{128,224},{160,192},{192,160},{224,1... | collective-permute-start | bytes 983048 | tf_op jit(solution)/shard_map/ppermute | solution.py:340
  57.2 4.1 %copy-start.5 = (bf16[128,640]{1,0:T(8,128)(2,1)}, bf16[128,640]{1,0:T(8,128)(2,1)S(1)}, u32[]{:S(2)}) copy-start(bf16[128,640]{1,0:T(8,128)(2,1)S(1)} %collective-permute-done.1.refs_2_) | copy-start | bytes 491524
  57.2 22.5 %collective-permute-start.6 = (bf16[128,1280]{1,0:T(8,128)(2,1)}, bf16[128,1280]{1,0:T(8,128)(2,1)}, u32[]{:S(2)}, u32[]{:S(2)}) collective-permute-start(bf16[128,1280]{1,0:T(8,128)(2,1)} %get-tuple-element.36), channel_id=1, source_target_pairs={{0,128},{32,160},{64,192},{96,224},{128,0},{160,32},{192,64},{224,... | collective-permute-start | bytes 983048 | tf_op jit(solution)/shard_map/ppermute | solution.py:340
  57.2 4.1 %copy-start.1 = (bf16[128,1280]{1,0:T(8,128)(2,1)}, bf16[128,1280]{1,0:T(8,128)(2,1)S(1)}, u32[]{:S(2)}) copy-start(bf16[128,1280]{1,0:T(8,128)(2,1)S(1)} %collective-permute-done.2.refs_3_) | copy-start | bytes 983044
  57.3 29.4 %collective-permute-start.7 = (bf16[128,1280]{1,0:T(8,128)(2,1)}, bf16[128,1280]{1,0:T(8,128)(2,1)}, u32[]{:S(2)}, u32[]{:S(2)}) collective-permute-start(bf16[128,1280]{1,0:T(8,128)(2,1)} %get-tuple-element.40), channel_id=1, source_target_pairs={{0,160},{32,128},{64,224},{96,192},{128,32},{160,0},{192,96},{224,... | collective-permute-start | bytes 983048 | tf_op jit(solution)/shard_map/ppermute | solution.py:340
  61.3 0.7 copy-start.2
  62.0 0.7 copy-start.3
  108.0 7.8 %collective-permute-start.8 = (bf16[80,128]{1,0:T(8,128)(2,1)S(1)}, bf16[80,128]{1,0:T(8,128)(2,1)S(1)}, u32[]{:S(2)}, u32[]{:S(2)}) collective-permute-start(bf16[80,128]{1,0:T(8,128)(2,1)S(1)} %reduce_sum.12), channel_id=1, source_target_pairs={{0,1},{1,0},{2,3},{3,2},{4,5},{5,4},{6,7},{7,6},{8,9},{9,8},{10,11... | collective-permute-start | bytes 61448 | tf_op jit(solution)/shard_map/ppermute | solution.py:286

commit v2 on v1

--- a/solution.py
+++ b/solution.py
@@ -37,7 +37,7 @@
 
 F32 = jnp.float32
 BF16 = jnp.bfloat16
-VMEM_LIMIT = 65000 * 1024
+VMEM_LIMIT = 40 * 1024 * 1024
 
 
 def contract_last(a, b):
@@ -86,6 +86,11 @@
 
 
 IN_VMEM = pl.BlockSpec(memory_space=pltpu.VMEM)
+ROOMY = pltpu.CompilerParams(vmem_limit_bytes=VMEM_LIMIT)
+
+
+def on_chip(a):
+    return pltpu.with_memory_space_constraint(a, pltpu.VMEM)
 
 
 def read_chunks(chunks, refs):
@@ -100,9 +105,6 @@
     return out
 
 
-ROOMY = pltpu.CompilerParams(vmem_limit_bytes=VMEM_LIMIT)
-
-
 def first_sequences(rows, weight, momentum, chunks):
     n = len(chunks)
     flat = [part for parts in chunks for part in parts]
@@ -116,7 +118,7 @@
         kernel,
         in_specs=[IN_VMEM] * (3 + len(flat)),
         out_specs=IN_VMEM,
-        out_shape=jax.ShapeDtypeStruct((LATENT, COLS_HERE), F32),
+        out_shape=pltpu.VMEM((LATENT, COLS_HERE), F32),
         compiler_params=ROOMY,
         name="first_sequences",
     )(rows, weight, momentum, *flat)
@@ -142,30 +144,24 @@
         in_specs=[IN_VMEM] * (3 + len(flat)),
         out_specs=(IN_VMEM,) * 4,
         out_shape=(
-            jax.ShapeDtypeStruct((LATENT, COLS_HERE), F32),
-            jax.ShapeDtypeStruct((SEQ, COLS_HERE), BF16),
-            jax.ShapeDtypeStruct((SEQ, LATENT + ROPE), BF16),
-            jax.ShapeDtypeStruct((LATENT, SEQ), BF16),
+            pltpu.VMEM((LATENT, COLS_HERE), F32),
+            pltpu.VMEM((SEQ, COLS_HERE), BF16),
+            pltpu.VMEM((SEQ, LATENT + ROPE), BF16),
+            pltpu.VMEM((LATENT, SEQ), BF16),
         ),
         compiler_params=ROOMY,
         name="middle_sequences",
-    )(rows, weight, sofar, *flat)
+    )(rows, weight, on_chip(sofar), *flat)
 
 
 def last_sequence(rows, turned, kv, sofar, chunk):
     half = LATENT // 2
     split_at = NT // 2
 
-    def kernel(rows_ref, turned_ref, kv_ref, chunk_ref, sofar_hbm, fresh_hbm, gram_ref, sofar_ref, fresh_ref, sems):
-        load = pltpu.make_async_copy(sofar_hbm, sofar_ref, sems.at[0])
-        load.start()
+    def kernel(rows_ref, turned_ref, kv_ref, chunk_ref, sofar_ref, fresh_ref, gram_ref):
         dkv = attend(rows_ref[...], kv_ref[...], [chunk_ref[...]])
-        add = dot(turned_ref[...], dkv)
-        load.wait()
-        fresh = (sofar_ref[...] + add).astype(BF16)
+        fresh = (sofar_ref[...] + dot(turned_ref[...], dkv)).astype(BF16)
         fresh_ref[...] = fresh
-        store = pltpu.make_async_copy(fresh_ref, fresh_hbm, sems.at[1])
-        store.start()
         top = contract_last(fresh[:half], fresh).astype(BF16)
         low = contract_last(fresh[half:], fresh[half:]).astype(BF16)
         for k, (a, b) in enumerate(PAIRS):
@@ -174,24 +170,18 @@
             else:
                 a, b = a - split_at, b - split_at
                 gram_ref[k] = low[a * TILE : (a + 1) * TILE, b * TILE : (b + 1) * TILE]
-        store.wait()
-
-    anywhere = pl.BlockSpec(memory_space=pl.ANY)
-    return pl.pallas_call(
-        kernel,
-        in_specs=[IN_VMEM] * 4 + [anywhere],
-        out_specs=(anywhere, IN_VMEM),
+
+    return pl.pallas_call(
+        kernel,
+        in_specs=[IN_VMEM] * 5,
+        out_specs=(IN_VMEM, IN_VMEM),
         out_shape=(
-            jax.ShapeDtypeStruct((LATENT, COLS_HERE), BF16),
-            jax.ShapeDtypeStruct((len(PAIRS), TILE, TILE), BF16),
+            pltpu.VMEM((LATENT, COLS_HERE), BF16),
+            pltpu.VMEM((len(PAIRS), TILE, TILE), BF16),
         ),
-        scratch_shapes=[
-            pltpu.VMEM((LATENT, COLS_HERE), F32),
-            pltpu.VMEM((LATENT, COLS_HERE), BF16),
-            pltpu.SemaphoreType.DMA((2,)),
-        ],
+        compiler_params=ROOMY,
         name="last_sequence",
-    )(rows, turned, kv, chunk, sofar)
+    )(*[on_chip(a) for a in (rows, turned, kv, chunk, sofar)])
 
 
 def split(a):
@@ -220,9 +210,9 @@
     parts = 4
     width = COLS_HERE // parts
 
-    def kernel(gram_ref, fresh_hbm, out_hbm, fresh_ref, base_ref, out_ref, sems):
-        load = pltpu.make_async_copy(fresh_hbm, fresh_ref, sems.at[0])
-        load.start()
+    def kernel(gram_ref, fresh_ref, out_hbm, momentum_hbm, base_ref, out_ref, sems):
+        stores = [pltpu.make_async_copy(fresh_ref, momentum_hbm, sems.at[parts])]
+        stores[0].start()
         on_diagonal = lax.broadcasted_iota(jnp.int32, (TILE, TILE), 0) == lax.broadcasted_iota(
             jnp.int32, (TILE, TILE), 1
         )
@@ -252,13 +242,11 @@
         later = first + poly_second * inner.astype(F32) + poly_third * dot(inner, inner)
         high, low = split(product(split(later), poly))
         factor = update_scale / norm
-        load.wait()
-        stores = []
         for k in range(parts):
             at = slice(k * width, (k + 1) * width)
             fresh = fresh_ref[:, at]
             out_ref[:, at] = (dot(high, fresh) + dot(low, fresh)) * factor
-            stores.append(pltpu.make_async_copy(out_ref.at[:, at], out_hbm.at[:, at], sems.at[1 + k]))
+            stores.append(pltpu.make_async_copy(out_ref.at[:, at], out_hbm.at[:, at], sems.at[k]))
             stores[-1].start()
         for store in stores:
             store.wait()
@@ -266,17 +254,20 @@
     anywhere = pl.BlockSpec(memory_space=pl.ANY)
     return pl.pallas_call(
         kernel,
-        in_specs=[IN_VMEM, anywhere],
-        out_specs=anywhere,
-        out_shape=jax.ShapeDtypeStruct((LATENT, COLS_HERE), F32),
+        in_specs=[IN_VMEM, IN_VMEM],
+        out_specs=(anywhere, anywhere),
+        out_shape=(
+            jax.ShapeDtypeStruct((LATENT, COLS_HERE), F32),
+            jax.ShapeDtypeStruct((LATENT, COLS_HERE), BF16),
+        ),
         scratch_shapes=[
-            pltpu.VMEM((LATENT, COLS_HERE), BF16),
             pltpu.VMEM((LATENT, LATENT), BF16),
             pltpu.VMEM((LATENT, COLS_HERE), F32),
-            pltpu.SemaphoreType.DMA((1 + parts,)),
+            pltpu.SemaphoreType.DMA((parts + 1,)),
         ],
+        compiler_params=ROOMY,
         name="update",
-    )(gram, fresh)
+    )(on_chip(gram), on_chip(fresh))
 
 
 def reduce_gram(gram):
@@ -370,7 +361,7 @@
         rows, weight, sofar, len(STEPS_FIRST), [chunks[s] for s in STEPS_MIDDLE]
     )
     fresh, gram = last_sequence(last_rows, turned, kv, sofar, chunks[STEP_LAST][0])
-    step = update(reduce_gram(gram), fresh)
+    step, fresh = update(reduce_gram(gram), fresh)
     return fresh[None], step[None]
 
 

time: 137 us -> 132 us (0.964)
  Pallas kernels: 28.1 us -> 19.2 us
  waiting for transfers between devices: 44.8 us -> 48 us
  local copies, waits for them, and re-layouts: 5.09 us -> 7.04 us
    pallas_call x2, Pallas kernels: 11.2 us -> 7.58 us  [the longest x1 5.26 us: update(): pl.pallas_call(kernel, in_specs=[IN_VMEM, IN_VMEM], out_specs=(anywhere,...]
    ppermute x8, waiting for transfers between devices: 36.9 us -> 40 us  [send(): return lax.ppermute(chunk, DP, [(k, k ^ s) for k in range(NDP)])]
    pallas_call x1, Pallas kernels: 5.28 us -> 2.58 us  [middle_sequences(): pl.pallas_call(kernel, in_specs=[IN_VMEM] * (3 + len(flat)), out_specs=(I...]
    pallas_call x1, Pallas kernels: 6.59 us -> 3.95 us  [first_sequences(): pl.pallas_call(kernel, in_specs=[IN_VMEM] * (3 + len(flat)), out_specs=IN...]
    unnamed x23 -> x33, local copies, waits for them, and re-layouts: 1.57 us -> 4.07 us
  transfers between devices with their start and end apart: 11 -> 11, of which waited for: 6 -> 6; matrix products, arithmetic and copies ran while one was open for 1% -> 1% of each run, Pallas kernels for 11% -> 7%
where the time goes in v2:
time: 132 us; the launch traced here: 130 us
  waiting for transfers between devices  48 us (36%)
  blocking collectives  28.1 us (21%)
  starting transfers between devices  26.4 us (20%)
  Pallas kernels  19.2 us (15%)
  local copies, waits for them, and re-layouts  7.04 us (5%)
    ppermute x8, waiting for transfers between devices, send(): return lax.ppermute(chunk, DP, [(k, k ^ s) for k in range(NDP)])  40 us
    all_to_all x1, blocking collectives, reduce_gram(): got = lax.all_to_all(pieces, YX, 0, 0, tiled=True)  16.1 us
    all_to_all x1, blocking collectives, reduce_gram(): lax.all_to_all(jnp.broadcast_to(mine[None], pieces.shape), YX, 0, 0, tile...  12 us
    ppermute x8, starting transfers between devices, send(): return lax.ppermute(chunk, DP, [(k, k ^ s) for k in range(NDP)])  8.6 us
    all_to_all x1, starting transfers between devices, inner_body(): lax.all_to_all(jnp.broadcast_to(rows[None], (NYX,) + rows.shape), YX, 0,...  7.08 us
    all_to_all x1, starting transfers between devices, inner_body(): rows = lax.all_to_all(rows, DP, 0, 0, tiled=True)  6.01 us
    pallas_call x1, Pallas kernels, update(): pl.pallas_call(kernel, in_specs=[IN_VMEM, IN_VMEM], out_specs=(anywhere,...  5.26 us
    pallas_call x2, Pallas kernels, pack(): pl.pallas_call(kernel, in_specs=[anywhere, anywhere], out_specs=[IN_VMEM]...  5.08 us
  transfers between devices with their start and end apart: 11, of which 6 were waited for; matrix products, arithmetic and copies ran while one was open for 1% of the time, Pallas kernels for 7%

profile of v2, /device:TPU:32, one launch (start us, length us, event | category | flops | bytes accessed | tf_op | source)
XLA Modules:
  0.0 130.4 jit_solution(2276813336985307512)
XLA Ops:
  0.7 1.8 %shard_map.77 = (bf16[128,640]{1,0:T(8,128)(2,1)}, bf16[128,640]{1,0:T(8,128)(2,1)}) custom-call(bf16[8,128,768]{2,1,0:T(8,128)(2,1)} %queries_ref.2, bf16[8,128,512]{2,1,0:T(8,128)(2,1)} %grads_ref.2), custom_call_target="tpu_custom_call" | custom-call | tf_op jit(solution)/shard_map/pallas_call | solution.py:321
  3.4 6.0 %all-to-all-start = ((bf16[8,8,576]{2,1,0:T(8,128)(2,1)}), bf16[8,8,576]{2,1,0:T(8,128)(2,1)S(1)}, u32[]{:S(2)}, u32[]{:S(2)}) async-start(bf16[8,8,576]{2,1,0:T(8,128)(2,1)} %pad_maximum_fusion), calls=%async_computation | async-start | bytes 163840 | tf_op jit(solution)/shard_map/all_to_all | solution.py:353
  9.4 4.9 %all-to-all-done = bf16[8,8,576]{2,1,0:T(8,128)(2,1)S(1)} async-done(((bf16[8,8,576]{2,1,0:T(8,128)(2,1)}), bf16[8,8,576]{2,1,0:T(8,128)(2,1)S(1)}, u32[]{:S(2)}, u32[]{:S(2)}) %all-to-all-start) | async-done | bytes 73760 | tf_op jit(solution)/shard_map/all_to_all | solution.py:353
  14.4 1.2 broadcast_in_dim.8
  15.6 7.1 %all-to-all-start.1 = ((bf16[16,8,8,576]{3,2,1,0:T(8,128)(2,1)}), bf16[16,8,8,576]{3,2,1,0:T(8,128)(2,1)}, u32[]{:S(2)}, u32[]{:S(2)}) async-start(bf16[16,8,8,576]{3,2,1,0:T(8,128)(2,1)} %broadcast_in_dim.8), calls=%async_computation.1 | async-start | bytes 2621440 | tf_op jit(solution)/shard_map/all_to_all | solution.py:355
  22.7 3.2 %shard_map.78 = (bf16[128,1280]{1,0:T(8,128)(2,1)}, bf16[128,1280]{1,0:T(8,128)(2,1)}, bf16[128,1280]{1,0:T(8,128)(2,1)}, bf16[128,1280]{1,0:T(8,128)(2,1)}, bf1...) custom-call(bf16[8,128,768]{2,1,0:T(8,128)(2,1)} %queries_ref.2, ...), custom_call_target="tpu_custom_call" | custom-call | tf_op jit(solution)/shard_map/pallas_call | solution.py:321
  26.1 1.0 collective-permute-start
  27.1 1.1 collective-permute-start.1
  28.2 3.5 %collective-permute-start.4 = (bf16[128,1280]{1,0:T(8,128)(2,1)}, bf16[128,1280]{1,0:T(8,128)(2,1)}, u32[]{:S(2)}, u32[]{:S(2)}) collective-permute-start(bf16[128,1280]{1,0:T(8,128)(2,1)} %get-tuple-element.36), channel_id=1, source_target_pairs={{0,64},{32,96},{64,0},{96,32},{128,192},{160,224},{192,128},{224,1... | collective-permute-start | bytes 983048 | tf_op jit(solution)/shard_map/ppermute | solution.py:331
  31.7 21.3 %collective-permute-done.refs_1_ = bf16[128,640]{1,0:T(8,128)(2,1)S(1)} collective-permute-done((bf16[128,640]{1,0:T(8,128)(2,1)S(1)}, bf16[128,640]{1,0:T(8,128)(2,1)S(1)}, u32[]{:S(2)}, u32[]{:S(2)}) %collective-permute-start) | collective-permute-done | bytes 163872 | tf_op jit(solution)/shard_map/ppermute | solution.py:331
  53.7 2.8 %collective-permute-done.1.refs_2_ = bf16[128,640]{1,0:T(8,128)(2,1)S(1)} collective-permute-done((bf16[128,640]{1,0:T(8,128)(2,1)S(1)}, bf16[128,640]{1,0:T(8,128)(2,1)S(1)}, u32[]{:S(2)}, u32[]{:S(2)}) %collective-permute-start.1) | collective-permute-done | bytes 163872 | tf_op jit(solution)/shard_map/ppermute | solution.py:331
  58.0 2.9 %collective-permute-start.7 = (bf16[128,1280]{1,0:T(8,128)(2,1)}, bf16[128,1280]{1,0:T(8,128)(2,1)}, u32[]{:S(2)}, u32[]{:S(2)}) collective-permute-start(bf16[128,1280]{1,0:T(8,128)(2,1)} %get-tuple-element.42), channel_id=1, source_target_pairs={{0,160},{32,128},{64,224},{96,192},{128,32},{160,0},{192,96},{224,... | collective-permute-start | bytes 983048 | tf_op jit(solution)/shard_map/ppermute | solution.py:331
  60.8 1.5 %copy_bitcast_fusion.rows_ref = bf16[8,128,576]{2,1,0:T(8,128)(2,1)S(1)} fusion(bf16[16,8,8,576]{3,2,1,0:T(8,128)(2,1)} %all-to-all-done.1), kind=kLoop, calls=%fused_computation | loop fusion | bytes 2359296 | tf_op jit(solution)/shard_map/reshape | solution.py:356
  62.4 1.0 copy-done.5
  64.3 3.9 %first_sequences.1.sofar_ref = f32[512,1024]{1,0:T(8,128)S(1)} custom-call(bf16[8,128,576]{2,1,0:T(8,128)(2,1)S(1)} %copy_bitcast_fusion.rows_ref, bf16[512,1024]{1,0:T(8,128)(2,1)S(1)} %bitcast.11, bf16[512,1024]{1,0:T(8,128)(2,1)S(1)} %bitcast.14, bf16[128,1280]{1,0:T(8,128)(2,1)S(1)} %copy-done.3, bf16[128,640]{1,0:T(8,128)(2,1)S(1)} %copy-done.7, ...), custom_call_target="tpu_custom_call" | custom-call | tf_op jit(solution)/shard_map/first_sequences/pallas_call | solution.py:117
  68.2 11.5 %collective-permute-done.6.refs_1_ = bf16[128,1280]{1,0:T(8,128)(2,1)} collective-permute-done((bf16[128,1280]{1,0:T(8,128)(2,1)}, bf16[128,1280]{1,0:T(8,128)(2,1)}, u32[]{:S(2)}, u32[]{:S(2)}) %collective-permute-start.6) | collective-permute-done | bytes 327712 | tf_op jit(solution)/shard_map/ppermute | solution.py:331
  79.8 2.6 %middle_sequences.1 = (f32[512,1024]{1,0:T(8,128)S(1)}, bf16[128,1024]{1,0:T(8,128)(2,1)S(1)}, bf16[128,576]{1,0:T(8,128)(2,1)S(1)}, bf16[512,128]{1,0:T(8,128)(2,1)S(1)}) custom-call(bf16[8,128,576]{2,1,0:T(8,128)(2,1)S(1)} %copy_bitcast_fusion.rows_ref, bf16[512,1024]{1,0:T(8,128)(2,1)S(1)} %bitcast.12, f32[512,1024]{1,0:T(8,128)S(1)} %first_sequences.1.sofar_ref, ...), custom_call_target="tpu_custom_call" | custom-call | tf_op jit(solution)/shard_map/middle_sequences/pallas_call | solution.py:142
  82.3 4.4 %collective-permute-done.7.chunk_ref = bf16[128,1280]{1,0:T(8,128)(2,1)} collective-permute-done((bf16[128,1280]{1,0:T(8,128)(2,1)}, bf16[128,1280]{1,0:T(8,128)(2,1)}, u32[]{:S(2)}, u32[]{:S(2)}) %collective-permute-start.7) | collective-permute-done | bytes 327712 | tf_op jit(solution)/shard_map/ppermute | solution.py:331
  86.7 2.3 %last_sequence.1 = (bf16[512,1024]{1,0:T(8,128)(2,1)S(1)}, bf16[10,128,128]{2,1,0:T(8,128)(2,1)S(1)}) custom-call(bf16[128,576]{1,0:T(8,128)(2,1)S(1)} %get-tuple-element.39.rows_ref, bf16[512,128]{1,0:T(8,128)(2,1)S(1)} %get-tuple-element.40.turned_ref, bf16[128,1024]{1,0:T(8,128)(2,1)S(1)} %get-tuple-element.41.kv_ref, ...), custom_call_target="tpu_custom_call" | custom-call | tf_op jit(solution)/shard_map/last_sequence/pallas_call | solution.py:174
  89.0 16.1 %all_to_all.20 = bf16[16,80,128]{2,1,0:T(8,128)(2,1)S(1)} all-to-all(bf16[16,80,128]{2,1,0:T(8,128)(2,1)S(1)} %bitcast.15), channel_id=1, replica_groups=mesh['zl'=4,'core'=2,'y'=4,'x'=4,'zh'=2] {'y','x'}, dimensions={0} | all-to-all | bytes 655360 | tf_op jit(solution)/shard_map/all_to_all | solution.py:275
  105.2 4.7 %collective-permute-start.8 = (bf16[80,128]{1,0:T(8,128)(2,1)S(1)}, bf16[80,128]{1,0:T(8,128)(2,1)S(1)}, u32[]{:S(2)}, u32[]{:S(2)}) collective-permute-start(bf16[80,128]{1,0:T(8,128)(2,1)S(1)} %reduce_sum.12), channel_id=1, source_target_pairs={{0,1},{1,0},{2,3},{3,2},{4,5},{5,4},{6,7},{7,6},{8,9},{9,8},{10,11... | collective-permute-start | bytes 61448 | tf_op jit(solution)/shard_map/ppermute | solution.py:277
  109.9 3.1 %collective-permute-done.8 = bf16[80,128]{1,0:T(8,128)(2,1)S(1)} collective-permute-done((bf16[80,128]{1,0:T(8,128)(2,1)S(1)}, bf16[80,128]{1,0:T(8,128)(2,1)S(1)}, u32[]{:S(2)}, u32[]{:S(2)}) %collective-permute-start.8) | collective-permute-done | bytes 20512 | tf_op jit(solution)/shard_map/ppermute | solution.py:277
  113.1 12.0 %all_to_all.21 = bf16[16,80,128]{2,1,0:T(8,128)(2,1)S(1)} all-to-all(bf16[16,80,128]{2,1,0:T(8,128)(2,1)S(1)} %broadcast_in_dim.9), channel_id=1, replica_groups=mesh['zl'=4,'core'=2,'y'=4,'x'=4,'zh'=2] {'y','x'}, dimensions={0} | all-to-all | bytes 655360 | tf_op jit(solution)/shard_map/all_to_all | solution.py:279
  125.0 5.3 %update.1 = (f32[512,1024]{1,0:T(8,128)}, bf16[512,1024]{1,0:T(8,128)(2,1)}) custom-call(bf16[10,128,128]{2,1,0:T(8,128)(2,1)S(1)} %bitcast.13, bf16[512,1024]{1,0:T(8,128)(2,1)S(1)} %get-tuple-element.45.fresh_ref), custom_call_target="tpu_custom_call" | custom-call | tf_op jit(solution)/shard_map/update/pallas_call | solution.py:255
  (49 shorter events, 4.2 us)
Async XLA Ops:
  0.6 1.9 %copy-start = (bf16[8,128,512]{2,1,0:T(8,128)(2,1)S(1)}, bf16[8,128,512]{2,1,0:T(8,128)(2,1)}, u32[]{:S(2)}) copy-start(bf16[8,128,512]{2,1,0:T(8,128)(2,1)} %param.6) | copy-start | bytes 3145732
  0.7 1.9 %copy-start.10 = (bf16[8,128,64]{1,2,0:T(8,128)(2,1)S(1)}, bf16[8,128,64]{1,2,0:T(8,128)(2,1)}, u32[]{:S(2)}) copy-start(bf16[8,128,64]{1,2,0:T(8,128)(2,1)} %param.7) | copy-start | bytes 393220
  3.4 10.9 %all-to-all-start = ((bf16[8,8,576]{2,1,0:T(8,128)(2,1)}), bf16[8,8,576]{2,1,0:T(8,128)(2,1)S(1)}, u32[]{:S(2)}, u32[]{:S(2)}) async-start(bf16[8,8,576]{2,1,0:T(8,128)(2,1)} %pad_maximum_fusion), calls=%async_computation | async-start | bytes 163840 | tf_op jit(solution)/shard_map/all_to_all | solution.py:353
  15.6 45.2 %all-to-all-start.1 = ((bf16[16,8,8,576]{3,2,1,0:T(8,128)(2,1)}), bf16[16,8,8,576]{3,2,1,0:T(8,128)(2,1)}, u32[]{:S(2)}, u32[]{:S(2)}) async-start(bf16[16,8,8,576]{3,2,1,0:T(8,128)(2,1)} %broadcast_in_dim.8), calls=%async_computation.1 | async-start | bytes 2621440 | tf_op jit(solution)/shard_map/all_to_all | solution.py:355
  22.7 3.4 %copy-start.12 = (bf16[128,640]{1,0:T(8,128)(2,1)S(1)}, bf16[128,640]{1,0:T(8,128)(2,1)}, u32[]{:S(2)}) copy-start(bf16[128,640]{1,0:T(8,128)(2,1)} %get-tuple-element.32) | copy-start | bytes 491524
  22.7 4.4 %copy-start.11 = (bf16[128,640]{1,0:T(8,128)(2,1)S(1)}, bf16[128,640]{1,0:T(8,128)(2,1)}, u32[]{:S(2)}) copy-start(bf16[128,640]{1,0:T(8,128)(2,1)} %get-tuple-element.33) | copy-start | bytes 491524
  26.0 31.3 %collective-permute-start.2 = (bf16[128,1280]{1,0:T(8,128)(2,1)}, bf16[128,1280]{1,0:T(8,128)(2,1)S(1)}, u32[]{:S(2)}, u32[]{:S(2)}) collective-permute-start(bf16[128,1280]{1,0:T(8,128)(2,1)} %get-tuple-element.34), channel_id=1, source_target_pairs={{0,224},{32,192},{64,160},{96,128},{128,96},{160,64},{192,32},{224... | collective-permute-start | bytes 983048 | tf_op jit(solution)/shard_map/ppermute | solution.py:331
  26.1 27.0 %collective-permute-start = (bf16[128,640]{1,0:T(8,128)(2,1)S(1)}, bf16[128,640]{1,0:T(8,128)(2,1)S(1)}, u32[]{:S(2)}, u32[]{:S(2)}) collective-permute-start(bf16[128,640]{1,0:T(8,128)(2,1)S(1)} %copy-done.12), channel_id=1, source_target_pairs={{0,192},{32,224},{64,128},{96,160},{128,64},{160,96},{192,0},{224,... | collective-permute-start | bytes 491528 | tf_op jit(solution)/shard_map/ppermute | solution.py:331
  27.1 29.4 %collective-permute-start.1 = (bf16[128,640]{1,0:T(8,128)(2,1)S(1)}, bf16[128,640]{1,0:T(8,128)(2,1)S(1)}, u32[]{:S(2)}, u32[]{:S(2)}) collective-permute-start(bf16[128,640]{1,0:T(8,128)(2,1)S(1)} %copy-done.11), channel_id=1, source_target_pairs={{0,192},{32,224},{64,128},{96,160},{128,64},{160,96},{192,0},{224,... | collective-permute-start | bytes 491528 | tf_op jit(solution)/shard_map/ppermute | solution.py:331
  28.2 34.1 %collective-permute-start.3 = (bf16[128,1280]{1,0:T(8,128)(2,1)}, bf16[128,1280]{1,0:T(8,128)(2,1)}, u32[]{:S(2)}, u32[]{:S(2)}) collective-permute-start(bf16[128,1280]{1,0:T(8,128)(2,1)} %get-tuple-element.35), channel_id=1, source_target_pairs={{0,32},{32,0},{64,96},{96,64},{128,160},{160,128},{192,224},{224,1... | collective-permute-start | bytes 983048 | tf_op jit(solution)/shard_map/ppermute | solution.py:331
  28.2 34.2 %collective-permute-start.4 = (bf16[128,1280]{1,0:T(8,128)(2,1)}, bf16[128,1280]{1,0:T(8,128)(2,1)}, u32[]{:S(2)}, u32[]{:S(2)}) collective-permute-start(bf16[128,1280]{1,0:T(8,128)(2,1)} %get-tuple-element.36), channel_id=1, source_target_pairs={{0,64},{32,96},{64,0},{96,32},{128,192},{160,224},{192,128},{224,1... | collective-permute-start | bytes 983048 | tf_op jit(solution)/shard_map/ppermute | solution.py:331
  53.0 0.7 copy-start.6
  53.7 14.5 %collective-permute-start.5 = (bf16[128,1280]{1,0:T(8,128)(2,1)}, bf16[128,1280]{1,0:T(8,128)(2,1)}, u32[]{:S(2)}, u32[]{:S(2)}) collective-permute-start(bf16[128,1280]{1,0:T(8,128)(2,1)} %get-tuple-element.37), channel_id=1, source_target_pairs={{0,96},{32,64},{64,32},{96,0},{128,224},{160,192},{192,160},{224,1... | collective-permute-start | bytes 983048 | tf_op jit(solution)/shard_map/ppermute | solution.py:331
  56.6 0.7 copy-start.8
  57.2 22.5 %collective-permute-start.6 = (bf16[128,1280]{1,0:T(8,128)(2,1)}, bf16[128,1280]{1,0:T(8,128)(2,1)}, u32[]{:S(2)}, u32[]{:S(2)}) collective-permute-start(bf16[128,1280]{1,0:T(8,128)(2,1)} %get-tuple-element.38), channel_id=1, source_target_pairs={{0,128},{32,160},{64,192},{96,224},{128,0},{160,32},{192,64},{224,... | collective-permute-start | bytes 983048 | tf_op jit(solution)/shard_map/ppermute | solution.py:331
  57.2 0.7 copy-start.4
  58.0 4.4 %copy-start.1 = (bf16[1,512,1024]{2,1,0:T(8,128)(2,1)S(1)}, bf16[1,512,1024]{2,1,0:T(8,128)(2,1)}, u32[]{:S(2)}) copy-start(bf16[1,512,1024]{2,1,0:T(8,128)(2,1)} %param.10) | copy-start | bytes 3145732
  58.0 4.4 %copy-start.2 = (bf16[1,512,1024]{2,1,0:T(8,128)(2,1)S(1)}, bf16[1,512,1024]{2,1,0:T(8,128)(2,1)}, u32[]{:S(2)}) copy-start(bf16[1,512,1024]{2,1,0:T(8,128)(2,1)} %param.11) | copy-start | bytes 3145732
  58.0 4.4 %copy-start.3 = (bf16[128,1280]{1,0:T(8,128)(2,1)S(1)}, bf16[128,1280]{1,0:T(8,128)(2,1)}, u32[]{:S(2)}) copy-start(bf16[128,1280]{1,0:T(8,128)(2,1)} %get-tuple-element.31.refs_0_) | copy-start | bytes 983044
  58.0 28.7 %collective-permute-start.7 = (bf16[128,1280]{1,0:T(8,128)(2,1)}, bf16[128,1280]{1,0:T(8,128)(2,1)}, u32[]{:S(2)}, u32[]{:S(2)}) collective-permute-start(bf16[128,1280]{1,0:T(8,128)(2,1)} %get-tuple-element.42), channel_id=1, source_target_pairs={{0,160},{32,128},{64,224},{96,192},{128,32},{160,0},{192,96},{224,... | collective-permute-start | bytes 983048 | tf_op jit(solution)/shard_map/ppermute | solution.py:331
  60.8 1.5 %copy-start.7 = (bf16[128,640]{1,0:T(8,128)(2,1)S(1)}, bf16[128,640]{1,0:T(8,128)(2,1)}, u32[]{:S(2)}) copy-start(bf16[128,640]{1,0:T(8,128)(2,1)} %copy-done.6) | copy-start | bytes 491524
  62.4 1.0 copy-start.5
  63.4 0.9 copy-start.9
  105.2 7.8 %collective-permute-start.8 = (bf16[80,128]{1,0:T(8,128)(2,1)S(1)}, bf16[80,128]{1,0:T(8,128)(2,1)S(1)}, u32[]{:S(2)}, u32[]{:S(2)}) collective-permute-start(bf16[80,128]{1,0:T(8,128)(2,1)S(1)} %reduce_sum.12), channel_id=1, source_target_pairs={{0,1},{1,0},{2,3},{3,2},{4,5},{5,4},{6,7},{7,6},{8,9},{9,8},{10,11... | collective-permute-start | bytes 61448 | tf_op jit(solution)/shard_map/ppermute | solution.py:277
